TPU v7x, 256 devices: a whole 4x4x8 slice. The times are simulated.
256 devices in a mesh: gx: 8 (over y, x_lo), gy: 32 (over x_hi, z, core).
Axes of the slice: x: 4 (x_hi: 2, x_lo: 2; x = x_hi * 2 + x_lo), y: 4, z: 8, core: 2. Of those that a mesh axis runs over, the one named last changes fastest.
Arguments:
- u_vel: float32 [8, 4096, 4096], P(None, 'gx', 'gy'), may hold values from -6 to 6
- v_vel: float32 [8, 4096, 4096], P(None, 'gx', 'gy'), may hold values from -6 to 6
- w_vel: float32 [8, 4096, 4096], P(None, 'gx', 'gy'), may hold values from -6 to 6
- thickness: float32 [8], replicated, may hold values from 128 to 512
Outputs:
- u_out: float32 [8, 4096, 4096], P(None, 'gx', 'gy')
- v_out: float32 [8, 4096, 4096], P(None, 'gx', 'gy')
- w_out: float32 [8, 4096, 4096], P(None, 'gx', 'gy')
All inputs are finite; a program needn't handle non-finite values.
Results may differ from a plain program's by a relative error of at most 0.0003.
Values sent between devices are 32-bit elements; how exact they have to be, the bound alone decides.
No kernel may reach another device: no remote copies, remote signals or barrier semaphores. Data moves between devices by JAX's collectives and lax.ppermute only.
A program may use at most 128 MiB of HBM per device.

v0:
```python
import math

import jax
import jax.numpy as jnp
from jax import lax
from jax.sharding import PartitionSpec as P

highest = lax.Precision.HIGHEST


def from_behind(block, axis, distance):
    devices = range(lax.axis_size(axis))
    route = [(i - distance, i) for i in devices if i - distance in devices]
    return lax.ppermute(block, axis, route)


def passed_along(shard, axis, by):
    length = lax.axis_size(axis)
    return lax.ppermute(shard, axis, [(i, (i + by) % length) for i in range(length)])


def spectra_tables(points):
    blocks = points // 128

    def angles(row_count, col_count, modulus):
        row_index = lax.broadcasted_iota(jnp.int32, (row_count, col_count), 0)
        col_index = lax.broadcasted_iota(jnp.int32, (row_count, col_count), 1)
        phase_angle = (row_index * col_index % modulus).astype(jnp.float32) * (
            2.0 * math.pi / modulus
        )
        return (jnp.cos(phase_angle), -jnp.sin(phase_angle))

    return (angles(blocks, blocks, blocks), angles(blocks, 128, points), angles(128, 128, 128))


def contract_pair(pattern, real_part, imag_part, table):
    cosine, sine_table = table

    def product_with(values, matrix):
        return jnp.einsum(pattern, values, matrix, precision=highest)

    if imag_part is None:
        return (product_with(real_part, cosine), product_with(real_part, sine_table))
    first_real = product_with(real_part, cosine) - product_with(imag_part, sine_table)
    first_imag = product_with(real_part, sine_table) + product_with(imag_part, cosine)
    return (first_real, first_imag)


def twiddle(real_part, imag_part, table, on_lanes):
    cosine, sine_table = table
    if on_lanes:
        cosine = cosine[:, :, None]
        sine_table = sine_table[:, :, None]
    return (
        real_part * cosine - imag_part * sine_table,
        real_part * sine_table + imag_part * cosine,
    )


def split_shape(data, on_lanes):
    if on_lanes:
        points = data.shape[-2]
        shaped = data.shape[:-2] + (points // 128, 128, data.shape[-1])
        forms = ("...abl,ac->...cbl", "...abl,bc->...acl")
    else:
        points = data.shape[-1]
        shaped = data.shape[:-1] + (points // 128, 128)
        forms = ("...ab,ac->...cb", "...ab,bc->...ac")
    return (points, shaped, forms)


def forward_transform(data, on_lanes):
    points, shaped, forms = split_shape(data, on_lanes)
    outer_table, middle, inner_table = spectra_tables(points)
    real_part, imag_part = contract_pair(forms[0], data.reshape(shaped), None, outer_table)
    real_part, imag_part = twiddle(real_part, imag_part, middle, on_lanes)
    real_part, imag_part = contract_pair(forms[1], real_part, imag_part, inner_table)
    return (real_part.reshape(data.shape), imag_part.reshape(data.shape))


def backward_transform(real_part, imag_part, on_lanes):
    points, shaped, forms = split_shape(real_part, on_lanes)
    outer_table, middle, inner_table = spectra_tables(points)
    imag_shaped = None if imag_part is None else imag_part.reshape(shaped)
    first_real, first_imag = contract_pair(
        forms[1], real_part.reshape(shaped), imag_shaped, inner_table
    )
    first_real, first_imag = twiddle(first_real, first_imag, middle, on_lanes)
    first_real, first_imag = contract_pair(forms[0], first_real, first_imag, outer_table)
    return (first_real.reshape(real_part.shape), first_imag.reshape(real_part.shape))


def natural_index(positions, points):
    return positions // 128 + points // 128 * (positions % 128)


def fold_phase(points):
    positions = jnp.arange(points, dtype=jnp.int32)
    angle = natural_index(positions, points).astype(jnp.float32) * (math.pi / (2 * points))
    return (jnp.cos(angle)[:, None], jnp.sin(angle)[:, None])


def level_solve(rhs, wave_x, wave_y, thickness, width_x, width_y):
    lam_x = -4.0 * jnp.sin(wave_x.astype(jnp.float32) * (math.pi / (2 * width_x))) ** 2
    lam_y = -4.0 * jnp.sin(wave_y.astype(jnp.float32) * (math.pi / width_y)) ** 2
    eigen = lam_x[:, None] + lam_y[None, :]
    ground = ((wave_x == 0)[:, None] & (wave_y == 0)[None, :]).astype(jnp.float32)
    centre = 0.5 * (thickness[:-1] + thickness[1:])
    upper = jnp.concatenate([1.0 / (thickness[:-1] * centre), jnp.zeros((1,), jnp.float32)])
    lower = jnp.concatenate([jnp.zeros((1,), jnp.float32), 1.0 / (thickness[1:] * centre)])
    above = jnp.concatenate([jnp.ones((1,), jnp.float32), upper[:-1]])
    pinned = jnp.concatenate([upper[:1], jnp.zeros((thickness.shape[0] - 1,), jnp.float32)])

    def sweep(carry, level):
        excess_prev, reduced_prev = carry
        lower_k, upper_k, above_k, pin_k, rhs_k = level
        excess = eigen - pin_k * ground + lower_k * excess_prev / (above_k - excess_prev)
        pivot_value = excess - upper_k
        reduced = (rhs_k - lower_k * reduced_prev) / pivot_value
        return ((excess, reduced), (reduced, upper_k / pivot_value))

    zeros_plane = jnp.zeros(eigen.shape, jnp.float32)
    unused, (reduced_all, ratio_all) = lax.scan(
        sweep, (zeros_plane, zeros_plane), (lower, upper, above, pinned, rhs)
    )

    def backward(carry, level):
        reduced, ratio = level
        value = reduced - ratio * carry
        return (value, value)

    unused_last, solved = lax.scan(backward, zeros_plane, (reduced_all, ratio_all), reverse=True)
    scale = (
        jnp.where(wave_x == 0, 1.0 / width_x, 2.0 / width_x).astype(jnp.float32)[:, None] / width_y
    )
    return solved * scale


def on_device(u_vel, v_vel, w_vel, thickness):
    levels, cells_x, cells_y = u_vel.shape
    parts_x = lax.axis_size("gx")
    parts_y = lax.axis_size("gy")
    index_x = lax.axis_index("gx")
    index_y = lax.axis_index("gy")
    width_x = cells_x * parts_x
    width_y = cells_y * parts_y
    global_x = index_x * cells_x + jnp.arange(cells_x, dtype=jnp.int32)
    at_wall = (global_x == width_x - 1)[None, :, None]
    zero_z = jnp.zeros((1, cells_x, cells_y), jnp.float32)
    u_open = jnp.where(at_wall, jnp.zeros((), jnp.float32), u_vel)
    west = from_behind(u_open[:, -1, :], "gx", 1)
    south = passed_along(v_vel[:, :, -1], "gy", 1)
    u_prev = jnp.concatenate([west[:, None, :], u_open[:, :-1, :]], axis=1)
    v_prev = jnp.concatenate([south[:, :, None], v_vel[:, :, :-1]], axis=2)
    w_open = jnp.concatenate([w_vel[:-1], zero_z], axis=0)
    w_prev = jnp.concatenate([zero_z, w_open[:-1]], axis=0)
    divergence = u_open - u_prev + (v_vel - v_prev) + (w_open - w_prev) / thickness[:, None, None]
    columns = lax.all_to_all(divergence, "gx", split_axis=0, concat_axis=1, tiled=True)
    slab = columns.shape[0]
    lines = columns.shape[2]
    paired = columns.reshape(slab, width_x // 2, 2, lines)
    folded = jnp.concatenate([paired[:, :, 0], jnp.flip(paired[:, :, 1], axis=1)], axis=1)
    real_part, imag_part = forward_transform(folded, True)
    cos_fold, sin_fold = fold_phase(width_x)
    along_x = real_part * cos_fold + imag_part * sin_fold
    rows = lax.all_to_all(along_x, "gy", split_axis=1, concat_axis=2, tiled=True)
    real_part, imag_part = forward_transform(rows, False)
    spectrum = real_part - imag_part
    span_x = width_x // parts_y
    base_x = index_y * span_x
    stacked = lax.all_to_all(spectrum, "gx", split_axis=2, concat_axis=0, tiled=True)
    span_y = width_y // parts_x
    wave_x = natural_index(base_x + jnp.arange(span_x, dtype=jnp.int32), width_x)
    wave_y = natural_index(index_x * span_y + jnp.arange(span_y, dtype=jnp.int32), width_y)
    pressure_hat = level_solve(stacked, wave_x, wave_y, thickness, width_x, width_y)
    back_rows = lax.all_to_all(pressure_hat, "gx", split_axis=0, concat_axis=2, tiled=True)
    real_part, imag_part = backward_transform(back_rows, None, False)
    pressure_rows = real_part - imag_part
    back_columns = lax.all_to_all(pressure_rows, "gy", split_axis=2, concat_axis=1, tiled=True)
    real_part, imag_part = backward_transform(
        back_columns * cos_fold, -(back_columns * sin_fold), True
    )
    half = width_x // 2
    evens = real_part[:, :half]
    odds = jnp.flip(real_part[:, half:], axis=1)
    pressure_cols = jnp.stack([evens, odds], axis=2).reshape(slab, width_x, lines)
    pressure = lax.all_to_all(pressure_cols, "gx", split_axis=1, concat_axis=0, tiled=True)
    east = from_behind(pressure[:, 0, :], "gx", -1)
    north = passed_along(pressure[:, :, 0], "gy", -1)
    next_x = jnp.concatenate([pressure[:, 1:, :], east[:, None, :]], axis=1)
    next_y = jnp.concatenate([pressure[:, :, 1:], north[:, :, None]], axis=2)
    next_z = jnp.concatenate([pressure[1:], zero_z], axis=0)
    centre = 0.5 * (thickness[:-1] + thickness[1:])
    spacing = jnp.concatenate([centre, jnp.ones((1,), jnp.float32)])
    u_out = jnp.where(at_wall, jnp.zeros((), jnp.float32), u_vel - (next_x - pressure))
    v_out = v_vel - (next_y - pressure)
    top = (jnp.arange(levels, dtype=jnp.int32) == levels - 1)[:, None, None]
    w_out = jnp.where(
        top, jnp.zeros((), jnp.float32), w_vel - (next_z - pressure) / spacing[:, None, None]
    )
    return (u_out, v_out, w_out)


def solution(mesh):
    return jax.shard_map(
        on_device,
        mesh=mesh,
        in_specs=(P(None, "gx", "gy"), P(None, "gx", "gy"), P(None, "gx", "gy"), P()),
        out_specs=(P(None, "gx", "gy"), P(None, "gx", "gy"), P(None, "gx", "gy")),
        check_vma=False,
    )
```

profile of v0, /device:TPU:41, one launch (start us, length us, event | category | flops | bytes accessed | tf_op | source)
XLA Modules:
  0.0 480.6 jit_solution(11567773257341767884)
XLA Ops:
  0.6 3.5 slice.64
  4.2 2.4 copy.329
  6.5 2.2 collective-permute-start.1
  10.2 3.1 collective-permute-start
  16.3 2.4 copy.392
  18.7 2.5 copy.391
  23.2 9.7 %fusion.8 = f32[8,512,128]{2,0,1:T(8,128)S(1)} fusion(f32[8,511,128]{2,0,1:T(8,128)} %slice.78, f32[8,1,128]{2,0,1:T(8,128)S(1)} %bitcast.277, f32[8,512,127]{2,0,1:T(8,128)} %copy.391, f32[8,512,1]{2,0,1:T(8,128)} %copy.264, f32[7,512,128]{2,0,1:T(8,128)} %copy.392, f32[8]{0:T(128)S(1)} %copy-done.5, pred[8]{0:T(512)(128)(4,1)S(1)} %copy-done.6, ...), kind=kLoop, calls=%fused_computation.16 | loop fusion | flops 5242880 | bytes 14418472 | tf_op jit(solution)/shard_map/add | solution.py:157
  34.6 5.0 %all-to-all-start = ((f32[8,512,128]{2,1,0:T(8,128)}), f32[8,512,128]{2,1,0:T(8,128)S(1)}, u32[]{:S(2)}, u32[]{:S(2)}) async-start(f32[8,512,128]{2,1,0:T(8,128)} %copy.268), calls=%async_computation | async-start | bytes 4194304 | tf_op jit(solution)/shard_map/all_to_all | solution.py:158
  40.1 24.9 %all-to-all-done = f32[8,512,128]{2,1,0:T(8,128)S(1)} async-done(((f32[8,512,128]{2,1,0:T(8,128)}), f32[8,512,128]{2,1,0:T(8,128)S(1)}, u32[]{:S(2)}, u32[]{:S(2)}) %all-to-all-start) | async-done | bytes 2097184 | tf_op jit(solution)/shard_map/all_to_all | solution.py:158
  65.0 2.4 fusion.285
  68.8 3.0 fusion.65
  71.8 3.9 multiply_subtract_fusion.1
  75.7 3.2 fusion.57
  78.9 3.4 fusion.55
  82.3 3.2 fusion.80
  85.5 3.2 fusion.83
  88.7 2.2 fusion.12
  90.9 62.3 %all_to_all.84 = f32[1,4096,128]{2,0,1:T(1,128)S(1)} all-to-all(f32[1,4096,128]{2,0,1:T(1,128)S(1)} %bitcast.263), channel_id=1, replica_groups=mesh['gx'=8,'gy'=32] {'gy'}, dimensions={1} | all-to-all | bytes 4194304 | tf_op jit(solution)/shard_map/all_to_all | solution.py:166
  153.2 3.0 fusion.29
  156.3 3.4 fusion.28
  159.7 3.4 fusion.45
  163.1 3.6 fusion.47
  166.6 3.4 fusion.49
  170.0 5.1 %add_subtract_fusion = f32[128,32,128]{0,2,1:T(8,128)} fusion(f32[128,32,128]{0,2,1:T(8,128)S(1)} %fusion.49, f32[128,32,128]{0,2,1:T(8,128)S(1)} %fusion.45, f32[128,32,128]{0,2,1:T(8,128)S(1)} %fusion.47, f32[128,32,128]{2,1,0:T(8,128)S(1)} %get-tuple-element.379), kind=kOutput, calls=%fused_computation.65 | convolution fusion | flops 807108608 | bytes 10485760 | tf_op jit(solution)/shard_map/...ab,bc->...ac/dot_general | solution.py:40
  175.1 5.0 %all-to-all-start.2 = ((f32[1,128,4096]{1,0,2:T(1,128)}), f32[1,128,4096]{1,0,2:T(1,128)S(1)}, u32[]{:S(2)}, u32[]{:S(2)}) async-start(f32[1,128,4096]{1,0,2:T(1,128)} %bitcast.32), calls=%async_computation.2 | async-start | bytes 4194304 | tf_op jit(solution)/shard_map/all_to_all | solution.py:171
  180.6 22.9 %all-to-all-done.2 = f32[1,128,4096]{1,0,2:T(1,128)S(1)} async-done(((f32[1,128,4096]{1,0,2:T(1,128)}), f32[1,128,4096]{1,0,2:T(1,128)S(1)}, u32[]{:S(2)}, u32[]{:S(2)}) %all-to-all-start.2) | async-done | bytes 2097184 | tf_op jit(solution)/shard_map/all_to_all | solution.py:171
  203.5 66.1 %while.34 = (s32[]{:T(128)}, f32[128,512]{1,0:T(8,128)S(1)}, f32[128,512]{1,0:T(8,128)S(1)}, f32[8,128,512]{2,1,0:T(8,128)}, f32[8,128,512]{2,1,0:T(8,128)}, /*i...) while((s32[]{:T(128)}, f32[128,512]{1,0:T(8,128)S(1)}, ...), condition=%wide.region_1.2_spmd.clone, body=%wide.region_0.1_spmd.clone.sunk | while | flops 1048579 | bytes 3153236 | solution.py:123
  206.0 3.5 bitcast_dynamic-update-slice_fusion.4
  209.6 2.1 bitcast_dynamic-update-slice_fusion.5
  214.3 3.5 bitcast_dynamic-update-slice_fusion.4
  217.9 2.1 bitcast_dynamic-update-slice_fusion.5
  222.5 3.5 bitcast_dynamic-update-slice_fusion.4
  226.2 2.1 bitcast_dynamic-update-slice_fusion.5
  230.8 3.5 bitcast_dynamic-update-slice_fusion.4
  234.4 2.1 bitcast_dynamic-update-slice_fusion.5
  239.0 3.5 bitcast_dynamic-update-slice_fusion.4
  242.7 2.1 bitcast_dynamic-update-slice_fusion.5
  247.3 3.5 bitcast_dynamic-update-slice_fusion.4
  250.9 2.1 bitcast_dynamic-update-slice_fusion.5
  255.5 3.5 bitcast_dynamic-update-slice_fusion.4
  259.2 2.1 bitcast_dynamic-update-slice_fusion.5
  263.8 3.5 bitcast_dynamic-update-slice_fusion.4
  267.4 2.1 bitcast_dynamic-update-slice_fusion.5
  269.7 11.1 %while.35 = (s32[]{:T(128)}, f32[128,512]{1,0:T(8,128)S(1)}, f32[8,128,512]{1,2,0:T(8,128)S(1)}, f32[8,128,512]{2,1,0:T(8,128)}, f32[8,128,512]{2,1,0:T(8,128)}, /*index=5*/s32[]{:T(128)}, s32[]{:T(128)}, s32[]{:T(128)}) while((s32[]{:T(128)}, f32[128,512]{1,0:T(8,128)S(1)}, f32[8,128,512]{1,2,0:T(8,128)S(1)}, ...), condition=%wide.region_3.4_spmd.clone, body=%wide.region_2.3_spmd.clone.sunk | while | flops 196612 | bytes 2097267 | solution.py:132
  280.9 30.6 %all_to_all.85 = f32[8,128,512]{1,2,0:T(8,128)S(1)} all-to-all(f32[8,128,512]{1,2,0:T(8,128)S(1)} %broadcast_multiply_fusion), channel_id=1, replica_groups=mesh['gx'=8,'gy'=32] {'gx'}, dimensions={0} | all-to-all | bytes 4194304 | tf_op jit(solution)/shard_map/all_to_all | solution.py:176
  311.6 3.6 fusion.103
  315.2 3.8 multiply_add_fusion
  318.9 3.0 fusion.37
  322.0 3.5 fusion.39
  325.5 3.0 fusion.41
  328.5 3.4 subtract_bitcast_fusion
  333.8 6.8 %all-to-all-start.4 = ((f32[1,128,4096]{1,0,2:T(1,128)}), f32[1,128,4096]{1,0,2:T(1,128)S(1)}, u32[]{:S(2)}, u32[]{:S(2)}) async-start(f32[1,128,4096]{1,0,2:T(1,128)} %bitcast.266), calls=%async_computation.4 | async-start | bytes 4194304 | tf_op jit(solution)/shard_map/all_to_all | solution.py:179
  340.8 52.0 %all-to-all-done.4 = f32[1,128,4096]{1,0,2:T(1,128)S(1)} async-done(((f32[1,128,4096]{1,0,2:T(1,128)}), f32[1,128,4096]{1,0,2:T(1,128)S(1)}, u32[]{:S(2)}, u32[]{:S(2)}) %all-to-all-start.4) | async-done | bytes 2097184 | tf_op jit(solution)/shard_map/all_to_all | solution.py:179
  397.1 2.3 fusion.74
  399.4 3.3 fusion.14
  402.7 3.3 fusion.33
  405.9 3.1 fusion.71
  411.0 8.6 %copy.303 = f32[1,2048,2,128]{3,2,1,0:T(2,128)} copy(f32[1,2048,2,128]{3,1,2,0:T(8,128)S(1)} %pad_maximum_fusion.1) | data formatting | bytes 4194304 | tf_op jit(solution)/shard_map/stack | solution.py:186
  419.5 5.1 %all-to-all-start.5 = ((f32[1,4096,128]{2,0,1:T(1,128)}), f32[1,4096,128]{2,0,1:T(1,128)S(1)}, u32[]{:S(2)}, u32[]{:S(2)}) async-start(f32[1,4096,128]{2,0,1:T(1,128)} %bitcast.265), calls=%async_computation.5 | async-start | bytes 4194304 | tf_op jit(solution)/shard_map/all_to_all | solution.py:187
  424.7 24.5 %all-to-all-done.5 = f32[1,4096,128]{2,0,1:T(1,128)S(1)} async-done(((f32[1,4096,128]{2,0,1:T(1,128)}), f32[1,4096,128]{2,0,1:T(1,128)S(1)}, u32[]{:S(2)}, u32[]{:S(2)}) %all-to-all-start.5) | async-done | bytes 2097184 | tf_op jit(solution)/shard_map/all_to_all | solution.py:187
  449.2 3.7 collective-permute-start.2
  455.6 2.4 collective-permute-start.3
  461.5 8.4 %subtract_select_fusion = (f32[8,512,128]{2,0,1:T(8,128)S(1)}, f32[8,512,128]{2,0,1:T(8,128)S(1)}) fusion(f32[7,512,128]{2,0,1:T(8,128)S(1)} %copy.310, f32[8]{0:T(128)S(1)} %pad_maximum_fusion.5, pred[8]{0:T(512)(128)(4,1)S(1)} %iota_compare_fusion, f32[8,512,128]{2,1,0:T(8,128)S(1)} %bitcast.249, f32[8,512,128]{2,1,0:T(8,128)S(1)} %copy-done.3, ...), kind=kLoop, calls=%fused_computation.60 | loop fusion | flops 4194304 | bytes 14418472 | tf_op jit(solution)/shard_map/jit(_where)/select_n | solution.py:198
  475.3 4.8 fusion.11
  (142 shorter events, 62.2 us)
Async XLA Ops:
  4.1 4.6 copy-start.1
  6.5 14.7 %collective-permute-start.1 = (f32[8,512]{1,0:T(8,128)S(1)}, f32[8,512]{1,0:T(8,128)S(1)}, u32[]{:S(2)}, u32[]{:S(2)}) collective-permute-start(f32[8,512]{1,0:T(8,128)S(1)} %bitcast.273), channel_id=1, source_target_pairs={{0,1},{1,2},{2,3},{3,4},{4,5},{5,6},{6,7},{7,8},{8,9},{9,10},{10,1... | collective-permute-start | bytes 49160 | tf_op jit(solution)/shard_map/ppermute | solution.py:19
  10.2 13.0 %collective-permute-start = (f32[8,128]{1,0:T(8,128)S(1)}, f32[8,128]{1,0:T(8,128)S(1)}, u32[]{:S(2)}, u32[]{:S(2)}) collective-permute-start(f32[8,128]{1,0:T(8,128)S(1)} %slice_bitcast_fusion.1), channel_id=1, source_target_pairs={{0,32},{32,64},{64,96},{96,128},{128,160},{160,192},{192,224},{1,3... | collective-permute-start | bytes 12296 | tf_op jit(solution)/shard_map/ppermute | solution.py:14
  14.8 1.5 slice-start
  16.3 2.4 copy-start
  21.2 2.0 copy-start.5
  21.2 2.0 copy-start.6
  34.6 30.3 %all-to-all-start = ((f32[8,512,128]{2,1,0:T(8,128)}), f32[8,512,128]{2,1,0:T(8,128)S(1)}, u32[]{:S(2)}, u32[]{:S(2)}) async-start(f32[8,512,128]{2,1,0:T(8,128)} %copy.268), calls=%async_computation | async-start | bytes 4194304 | tf_op jit(solution)/shard_map/all_to_all | solution.py:158
  67.4 1.2 copy-start.4
  175.1 28.4 %all-to-all-start.2 = ((f32[1,128,4096]{1,0,2:T(1,128)}), f32[1,128,4096]{1,0,2:T(1,128)S(1)}, u32[]{:S(2)}, u32[]{:S(2)}) async-start(f32[1,128,4096]{1,0,2:T(1,128)} %bitcast.32), calls=%async_computation.2 | async-start | bytes 4194304 | tf_op jit(solution)/shard_map/all_to_all | solution.py:171
  333.8 59.0 %all-to-all-start.4 = ((f32[1,128,4096]{1,0,2:T(1,128)}), f32[1,128,4096]{1,0,2:T(1,128)S(1)}, u32[]{:S(2)}, u32[]{:S(2)}) async-start(f32[1,128,4096]{1,0,2:T(1,128)} %bitcast.266), calls=%async_computation.4 | async-start | bytes 4194304 | tf_op jit(solution)/shard_map/all_to_all | solution.py:179
  419.5 29.7 %all-to-all-start.5 = ((f32[1,4096,128]{2,0,1:T(1,128)}), f32[1,4096,128]{2,0,1:T(1,128)S(1)}, u32[]{:S(2)}, u32[]{:S(2)}) async-start(f32[1,4096,128]{2,0,1:T(1,128)} %bitcast.265), calls=%async_computation.5 | async-start | bytes 4194304 | tf_op jit(solution)/shard_map/all_to_all | solution.py:187
  449.2 11.3 %collective-permute-start.2 = (f32[8,128]{1,0:T(8,128)S(1)}, f32[8,128]{1,0:T(8,128)S(1)}, u32[]{:S(2)}, u32[]{:S(2)}) collective-permute-start(f32[8,128]{1,0:T(8,128)S(1)} %bitcast.278), channel_id=1, source_target_pairs={{32,0},{64,32},{96,64},{128,96},{160,128},{192,160},{224,192},{33,... | collective-permute-start | bytes 12296 | tf_op jit(solution)/shard_map/ppermute | solution.py:14
  455.6 17.8 %collective-permute-start.3 = (f32[8,512]{1,0:T(8,128)S(1)}, f32[8,512]{1,0:T(8,128)S(1)}, u32[]{:S(2)}, u32[]{:S(2)}) collective-permute-start(f32[8,512]{1,0:T(8,128)S(1)} %slice_reduce_fusion), channel_id=1, source_target_pairs={{0,31},{1,0},{2,1},{3,2},{4,3},{5,4},{6,5},{7,6},{8,7},{9,8},{10,9... | collective-permute-start | bytes 49160 | tf_op jit(solution)/shard_map/ppermute | solution.py:19
  459.3 1.6 copy-start.3
  459.4 2.1 copy-start.2
where the time goes:
time: 489 us; the launch traced here: 481 us
  waiting for transfers between devices  124 us (25%)
  blocking collectives  93 us (19%)
  other arithmetic  82.2 us (17%)
  matrix products  78.1 us (16%)
  local copies, waits for them, and re-layouts  67.5 us (14%)
  starting transfers between devices  33.5 us (7%)
    dot_general x24, matrix products, product_with(): return jnp.einsum(pattern, values, matrix, precision=highest)  78.1 us
    all_to_all x1, blocking collectives, on_device(): lax.all_to_all(along_x, 'gy', split_axis=1, concat_axis=2, tiled=True)  62.3 us
    all_to_all x1, waiting for transfers between devices, on_device(): lax.all_to_all(pressure_rows, 'gy', split_axis=2, concat_axis=1, tiled=True)  52 us
    dynamic_update_slice x16, other arithmetic, level_solve(): lax.scan(sweep, (zeros_plane, zeros_plane), (lower, upper, above, pinned,...  44.9 us
    all_to_all x1, blocking collectives, on_device(): lax.all_to_all(pressure_hat, 'gx', split_axis=0, concat_axis=2, tiled=True)  30.6 us
    all_to_all x1, waiting for transfers between devices, on_device(): lax.all_to_all(divergence, 'gx', split_axis=0, concat_axis=1, tiled=True)  24.9 us
    all_to_all x1, waiting for transfers between devices, on_device(): lax.all_to_all(pressure_cols, 'gx', split_axis=1, concat_axis=0, tiled=True)  24.5 us
    all_to_all x1, waiting for transfers between devices, on_device(): lax.all_to_all(spectrum, 'gx', split_axis=2, concat_axis=0, tiled=True)  22.9 us
  transfers between devices with their start and end apart: 8, of which 4 were waited for; matrix products, arithmetic and copies ran while one was open for 6% of the time, Pallas kernels for 0%

commit v1 on v0

v1 whole, which is shorter than its diff:
```python
import math

import jax
import jax.numpy as jnp
import numpy as np
from jax import lax
from jax.experimental import pallas as pl
from jax.experimental.pallas import tpu as pltpu
from jax.sharding import PartitionSpec as P

highest = lax.Precision.HIGHEST
f32 = jnp.float32
NX = 4096
NY = 4096
NZ = 8
LX = 512
ROWS = 136
PAY = 520
HALF = float(np.sqrt(0.5))

CLASSES = [0] + [mu + 16 * tau for mu in range(1, 8) for tau in range(4)] + [16, 8, 24]


def class_modes():
    t = np.arange(64)
    rows = [np.concatenate([64 * t, 64 * t + 32])]
    for nu in CLASSES[1:]:
        rows.append(np.concatenate([64 * t + nu, 64 * (t + 1) - nu]))
    return np.stack(rows)


def dct_tables():
    b = np.arange(128)[:, None]
    t = np.arange(64)[None, :]
    near = math.pi * t * (2 * b + 1) / 128
    far = math.pi * (t + 1) * (2 * b + 1) / 128
    common = np.block([[np.cos(near), np.cos(far)], [np.sin(near), -np.sin(far)]])
    zero = np.zeros((128, 64))
    middle = np.cos(math.pi * (64 * t + 32) * (2 * b + 1) / 8192)
    first = np.block([[np.cos(near), zero], [zero, middle]])
    nu = np.array(CLASSES)[:, None]
    angle = math.pi * nu * (2 * np.arange(128)[None, :] + 1) / 8192
    return common, first, np.cos(angle), np.sin(angle)


def line_tables():
    d = np.arange(32)
    j = np.arange(128)
    a32 = 2 * math.pi * (d[:, None] * d[None, :] % 32) / 32
    a128 = 2 * math.pi * (j[:, None] * j[None, :] % 128) / 128
    tw = 2 * math.pi * (d[:, None] * j[None, :]) / 4096
    q = d[:, None] + 32 * j[None, :]
    lam = -4.0 * np.sin(math.pi * q / NY) ** 2
    return np.cos(a32), np.sin(a32), np.cos(tw), np.sin(tw), np.cos(a128), np.sin(a128), lam


def const(values):
    return jnp.asarray(np.asarray(values, dtype=np.float32))


def across_blocks(x):
    e = [x[s] + x[s + 4] for s in range(4)]
    o = [x[s] - x[s + 4] for s in range(4)]
    out = [None] * 9
    e02, e13 = e[0] + e[2], e[1] + e[3]
    out[0] = e02 + e13
    out[8] = e02 - e13
    out[4] = (e[0] - e[2], e[3] - e[1])
    d13, s13 = HALF * (o[1] - o[3]), HALF * (o[1] + o[3])
    out[2] = (o[0] + d13, -o[2] - s13)
    out[6] = (o[0] - d13, o[2] - s13)
    zr, zi = [x[0]], [-x[4]]
    for s in (1, 2, 3):
        c, q = math.cos(math.pi * s / 8), math.sin(math.pi * s / 8)
        zr.append(x[s] * c - x[s + 4] * q)
        zi.append(-(x[s] * q + x[s + 4] * c))
    y = four(zr, zi)
    out[1] = y[0]
    out[5] = y[1]
    out[7] = (y[2][0], -y[2][1])
    out[3] = (y[3][0], -y[3][1])
    return out


def four(zr, zi):
    t0r, t0i = zr[0] + zr[2], zi[0] + zi[2]
    t1r, t1i = zr[0] - zr[2], zi[0] - zi[2]
    t2r, t2i = zr[1] + zr[3], zi[1] + zi[3]
    t3r, t3i = zr[1] - zr[3], zi[1] - zi[3]
    return [
        (t0r + t2r, t0i + t2i),
        (t1r + t3i, t1i - t3r),
        (t0r - t2r, t0i - t2i),
        (t1r - t3i, t1i + t3r),
    ]


def four_back(h):
    zr = [v[0] for v in h]
    zi = [v[1] for v in h]
    t0r, t0i = zr[0] + zr[2], zi[0] + zi[2]
    t1r, t1i = zr[0] - zr[2], zi[0] - zi[2]
    t2r, t2i = zr[1] + zr[3], zi[1] + zi[3]
    t3r, t3i = zr[1] - zr[3], zi[1] - zi[3]
    return [
        (t0r + t2r, t0i + t2i),
        (t1r - t3i, t1i + t3r),
        (t0r - t2r, t0i - t2i),
        (t1r + t3i, t1i - t3r),
    ]


def forward_classes(x):
    per_a = [across_blocks([x[4 * s + a] for s in range(8)]) for a in range(4)]
    out = []
    y0 = [per_a[a][0] for a in range(4)]
    y8 = [per_a[a][8] for a in range(4)]
    out.append(((y0[0] + y0[2]) + (y0[1] + y0[3]), (y0[0] + y0[2]) - (y0[1] + y0[3])))
    for mu in range(1, 8):
        zr, zi = [per_a[0][mu][0]], [per_a[0][mu][1]]
        for a in (1, 2, 3):
            yr, yi = per_a[a][mu]
            c, q = math.cos(math.pi * mu * a / 32), math.sin(math.pi * mu * a / 32)
            zr.append(yr * c + yi * q)
            zi.append(yi * c - yr * q)
        out.extend(four(zr, zi))
    out.append((y0[0] - y0[2], y0[3] - y0[1]))
    d13, s13 = HALF * (y8[1] - y8[3]), HALF * (y8[1] + y8[3])
    out.append((y8[0] + d13, -y8[2] - s13))
    out.append((y8[0] - d13, y8[2] - s13))
    return out


def backward_classes(h):
    h0, h32 = h[0]
    h16, h8, h24 = h[29], h[30], h[31]
    x = [None] * 32
    by_mu = {}
    for mu in range(1, 8):
        z = four_back(h[1 + 4 * (mu - 1) : 5 + 4 * (mu - 1)])
        for a in (1, 2, 3):
            c, q = math.cos(math.pi * mu * a / 32), math.sin(math.pi * mu * a / 32)
            zr, zi = z[a]
            z[a] = (zr * c - zi * q, zr * q + zi * c)
        by_mu[mu] = z
    sum0, dif0 = h0 + h32, h0 - h32
    y0 = [sum0 + h16[0], dif0 - h16[1], sum0 - h16[0], dif0 + h16[1]]
    dr, di = HALF * (h8[0] - h24[0]), HALF * (h8[1] + h24[1])
    y8 = [h8[0] + h24[0], dr - di, h24[1] - h8[1], -dr - di]
    for a in range(4):
        y = {mu: by_mu[mu][a] for mu in by_mu}
        ea, eb = y0[a] + y8[a], y0[a] - y8[a]
        y2, y4, y6 = y[2], y[4], y[6]
        rep = [ea + y4[0], eb - y4[1], ea - y4[0], eb + y4[1]]
        er, ei = HALF * (y2[0] - y6[0]), HALF * (y2[1] + y6[1])
        alt = [y2[0] + y6[0], er - ei, y6[1] - y2[1], -er - ei]
        u = four_back([y[1], y[5], (y[7][0], -y[7][1]), (y[3][0], -y[3][1])])
        for s in range(4):
            ur, ui = u[s]
            if s:
                c, q = math.cos(math.pi * s / 8), math.sin(math.pi * s / 8)
                ur, ui = ur * c - ui * q, ur * q + ui * c
            x[4 * s + a] = rep[s] + alt[s] + ur
            x[4 * (s + 4) + a] = rep[s] - alt[s] - ui
    return x


def decay(eigen):
    half = 0.5 * jnp.sqrt(-eigen)
    root = jnp.sqrt(1.0 + half * half)
    gap = 2.0 * half * (root - half)
    return 1.0 - gap, gap, -0.25 / (half * root)


def doubled(gap, times):
    for _ in range(times):
        gap = gap * (2.0 - gap)
    return gap


ROUNDS = []
_seats = list(range(8))
for _ in range(7):
    ROUNDS.append([tuple(sorted((_seats[i], _seats[7 - i]))) for i in range(4)])
    _seats = [_seats[0], _seats[7]] + _seats[1:7]
SWEEPS = 6
PAIRS = [(i, j) for i in range(8) for j in range(i, 8)]


def vertical_modes(thick_ref, mix_ref, unmix_ref, mu_ref):
    t = [jnp.full((8, 128), thick_ref[k], f32) for k in range(8)]
    unit = 16384.0
    zero = jnp.zeros((8, 128), f32)
    one = jnp.ones((8, 128), f32)
    centre = [0.5 * (t[k] + t[k + 1]) for k in range(7)]
    root = [jnp.sqrt(t[k]) for k in range(8)]
    a = {pair: zero for pair in PAIRS}
    for k in range(8):
        total = zero
        if k < 7:
            total = total + unit / (t[k] * centre[k])
            a[(k, k + 1)] = unit / (centre[k] * (root[k] * root[k + 1]))
        if k > 0:
            total = total + unit / (t[k] * centre[k - 1])
        a[(k, k)] = -total
    vec = [[one if i == j else zero for j in range(8)] for i in range(8)]

    def sweep(_, carry):
        flat_a, flat_v = carry
        a = dict(zip(PAIRS, flat_a))
        vec = [list(flat_v[8 * i : 8 * i + 8]) for i in range(8)]

        def get(i, j):
            return a[(i, j) if i <= j else (j, i)]

        for pairs in ROUNDS:
            turn = {}
            for p, q in pairs:
                off = a[(p, q)]
                diff = a[(q, q)] - a[(p, p)]
                size = jnp.sqrt(diff * diff + 4.0 * off * off)
                low = jnp.where(diff < 0.0, diff - size, diff + size)
                tan = 2.0 * off / jnp.where(low == 0.0, 1.0, low)
                cos = 1.0 / jnp.sqrt(1.0 + tan * tan)
                turn[(p, q)] = (cos, tan * cos, tan)
            full = [[get(i, j) for j in range(8)] for i in range(8)]
            for p, q in pairs:
                cos, sin, _t = turn[(p, q)]
                for i in range(8):
                    x, y = full[i][p], full[i][q]
                    full[i][p], full[i][q] = cos * x - sin * y, sin * x + cos * y
                    x, y = vec[i][p], vec[i][q]
                    vec[i][p], vec[i][q] = cos * x - sin * y, sin * x + cos * y
            for p, q in pairs:
                cos, sin, tan = turn[(p, q)]
                for j in range(8):
                    x, y = full[p][j], full[q][j]
                    full[p][j], full[q][j] = cos * x - sin * y, sin * x + cos * y
            diag = {}
            for p, q in pairs:
                cos, sin, tan = turn[(p, q)]
                off = a[(p, q)]
                diag[p] = a[(p, p)] - tan * off
                diag[q] = a[(q, q)] + tan * off
            a = {(i, j): full[i][j] for i, j in PAIRS}
            for p, q in pairs:
                a[(p, q)] = zero
            for p in diag:
                a[(p, p)] = diag[p]
        return tuple(a[pair] for pair in PAIRS), tuple(vec[i][j] for i in range(8) for j in range(8))

    start = (tuple(a[pair] for pair in PAIRS), tuple(vec[i][j] for i in range(8) for j in range(8)))
    flat_a, flat_v = lax.fori_loop(0, SWEEPS, sweep, start)
    a = dict(zip(PAIRS, flat_a))
    for mode in range(8):
        mu_ref[mode : mode + 1, :] = jnp.minimum(a[(mode, mode)] * (1.0 / unit), 0.0)[0:1]
        for k in range(8):
            entry = flat_v[8 * k + mode]
            mix_ref[8 * mode + k : 8 * mode + k + 1, :] = (entry * root[k])[0:1]
            unmix_ref[8 * k + mode : 8 * k + mode + 1, :] = (entry / root[k])[0:1]


def iota(shape, axis):
    return lax.broadcasted_iota(jnp.int32, shape, axis)


def divergence_kernel(gx_ref, thick_ref, mix_ref, u_ref, v_ref, w_ref, out_ref, last_ref, sum_ref):
    step = pl.program_id(0)
    wall = jnp.logical_and(gx_ref[0] == 7, step == 3)

    @pl.when(step == 0)
    def _():
        last_ref[...] = jnp.zeros((64, 128), f32)
        sum_ref[...] = jnp.zeros((64, 128), f32)

    lane = iota((16, 128), 1)
    row = iota((16, 128), 0)
    ones = jnp.ones((1, 128), f32)
    inverse = [1.0 / (ones * thick_ref[k]) for k in range(8)]
    base = pl.multiple_of(step * 128, 128)
    for sub in range(8):
        rows = slice(16 * sub, 16 * sub + 16)
        div = []
        below = None
        for k in range(8):
            u = u_ref[k, rows, :]
            if sub == 7:
                u = jnp.where(jnp.logical_and(wall, row == 15), 0.0, u)
            prev = pltpu.roll(u, 1, axis=0)
            prev = jnp.where(row == 0, last_ref[8 * k : 8 * k + 1, :], prev)
            last_ref[8 * k : 8 * k + 1, :] = u[15:16]
            v = v_ref[k, rows, :]
            back = jnp.where(lane == 0, 0.0, pltpu.roll(v, 1, axis=1))
            if k < 7:
                w = w_ref[k, rows, :]
                up = w if below is None else w - below
                below = w
            else:
                up = -below
            rise = up * inverse[k]
            sum_ref[8 * k : 8 * k + 8, :] += rise[0:8] + rise[8:16]
            div.append((u - prev) + (v - back) + rise)
        for mode in range(8):
            acc = div[0] * mix_ref[8 * mode : 8 * mode + 1, :]
            for k in range(1, 8):
                acc = acc + div[k] * mix_ref[8 * mode + k : 8 * mode + k + 1, :]
            out_ref[mode, pl.ds(base + 16 * sub, 16), :] = acc

    lanes = iota((128, 128), 1)
    edge = jnp.zeros((128, 128), f32)
    for k in range(8):
        edge = jnp.where(lanes == k, pltpu.roll(v_ref[k], k + 1, axis=1), edge)
    edge = edge.T
    for mode in range(8):
        acc = edge[0:1] * mix_ref[8 * mode : 8 * mode + 1, :]
        for k in range(1, 8):
            acc = acc + edge[k : k + 1] * mix_ref[8 * mode + k : 8 * mode + k + 1, :]
        out_ref[mode, pl.ds(513 + step, 1), :] = -acc

    @pl.when(step == 3)
    def _():
        lane1 = iota((1, 128), 1)
        totals = jnp.zeros((1, 128), f32)
        for k in range(8):
            part = jnp.sum(sum_ref[8 * k : 8 * k + 8, :], axis=0, keepdims=True)
            part = jnp.sum(part, axis=1, keepdims=True)
            totals = jnp.where(lane1 == k, part, totals)
        for mode in range(8):
            acc = last_ref[0:1, :] * mix_ref[8 * mode : 8 * mode + 1, :]
            for k in range(1, 8):
                acc = acc + last_ref[8 * k : 8 * k + 1, :] * mix_ref[8 * mode + k : 8 * mode + k + 1, :]
            out_ref[mode, 512:513, :] = acc
            out_ref[mode, 517:518, :] = totals
            out_ref[mode, 518:520, :] = jnp.zeros((2, 128), f32)


def eigen_table(sines, mu_row, with_first):
    eigen = mu_row - 4.0 * sines
    if with_first:
        first = jnp.logical_and(iota(sines.shape, 0) == 0, iota(sines.shape, 1) == 0)
        eigen = jnp.where(first, -1.0, eigen)
    return eigen


def forward_kernel(
    gx_ref, mu_ref, sines_ref, tc_ref, ts_ref, common_ref, first_ref, in_ref, out_ref, small_ref,
    grid_ref, y_ref, side_ref,
):
    row8 = iota((8, 128), 0)
    row128 = iota((128, 128), 0)
    for s in range(8):
        for part in range(4):
            tile = in_ref[s, 128 * part : 128 * part + 128, :]
            if part == 0 and s > 0:
                tile = jnp.where(row128 == 0, tile - in_ref[s - 1, 512:513, :], tile)
            grid_ref[4 * s + part, 0:128, :] = tile.T
            ghost = in_ref[s, 513 + part : 514 + part, :]
            grid_ref[4 * s + part, 128:136, :] = jnp.where(row8 == 0, ghost, 0.0)

    def group(i, carry):
        start = pl.multiple_of(i * 8, 8)
        rows = pl.ds(start, 8)
        y = forward_classes([grid_ref[g, rows, :] for g in range(32)])
        y_ref[0, rows, 0:128] = y[0][0]
        y_ref[0, rows, 128:256] = y[0][1]
        for c in range(1, 32):
            re, im = y[c]
            tc, ts = tc_ref[c : c + 1, :], ts_ref[c : c + 1, :]
            y_ref[c, rows, 0:128] = re * tc + im * ts
            y_ref[c, rows, 128:256] = im * tc - re * ts
        return carry

    lax.fori_loop(0, ROWS // 8, group, 0)

    out_ref[0:ROWS, :] = jnp.dot(y_ref[0], first_ref[...], precision=highest, preferred_element_type=f32)

    def product(c, carry):
        start = pl.multiple_of(c * ROWS, 8)
        out_ref[pl.ds(start, ROWS), :] = jnp.dot(
            y_ref[c], common_ref[...], precision=highest, preferred_element_type=f32
        )
        return carry

    lax.fori_loop(1, 32, product, 0)

    line = out_ref[0:128, :].T[0:1]
    ghost_line = out_ref[128:129, :]

    eigen = eigen_table(sines_ref[...], mu_ref[pl.ds(gx_ref[0], 1), :], True)
    rho, gap, _ = decay(eigen)
    ghost = out_ref[pl.ds(128, 32, stride=ROWS), :]

    def from_north(n, b):
        j = 127 - n
        side_ref[pl.ds(j, 32, stride=ROWS), :] = rho * b
        return out_ref[pl.ds(j, 32, stride=ROWS), :] + (b - gap * b)

    b = lax.fori_loop(0, 128, from_north, ghost, unroll=8)

    def from_south(j, f):
        f = out_ref[pl.ds(j, 32, stride=ROWS), :] + (f - gap * f)
        out_ref[pl.ds(j, 32, stride=ROWS), :] = f + side_ref[pl.ds(j, 32, stride=ROWS), :]
        return f

    f = lax.fori_loop(0, 128, from_south, jnp.zeros((32, 128), f32), unroll=8)
    out_ref[pl.ds(128, 32, stride=ROWS), :] = rho * f + ghost

    totals = in_ref[0, 517:518, :]
    for s in range(1, 8):
        totals = totals + in_ref[s, 517:518, :]
    small_ref[pl.ds(0, 32, stride=8), :] = f + ghost / rho
    small_ref[pl.ds(1, 32, stride=8), :] = b
    small_ref[pl.ds(2, 32, stride=8), :] = jnp.broadcast_to(line, (32, 128))
    small_ref[pl.ds(3, 32, stride=8), :] = jnp.broadcast_to(totals, (32, 128))
    small_ref[pl.ds(4, 32, stride=8), :] = jnp.broadcast_to(ghost_line, (32, 128))
    for r in (5, 6, 7):
        small_ref[pl.ds(r, 32, stride=8), :] = jnp.zeros((32, 128), f32)


def carry_kernel(gx_ref, gy_ref, mu_ref, sines_ref, in_ref, out_ref):
    own = gy_ref[0]
    eigen = mu_ref[pl.ds(gx_ref[0], 1), :] - 4.0 * sines_ref[pl.ds(own, 1), :]
    first = jnp.logical_and(own == 0, iota((1, 128), 1) == 0)
    eigen = jnp.where(first, -1.0, eigen)
    _, gap, _ = decay(eigen)
    gap_block = doubled(gap, 7)
    around = 1.0 / doubled(gap_block, 5)
    c = jnp.zeros((1, 128), f32)
    h = jnp.zeros((1, 128), f32)
    for d in range(32):
        c = in_ref[8 * d : 8 * d + 1, :] + (c - gap_block * c)
        e = 31 - d
        h = in_ref[8 * e + 1 : 8 * e + 2, :] + (h - gap_block * h)
    c = c * around
    h = h * around
    out_ref[...] = jnp.zeros((256, 128), f32)
    for d in range(32):
        out_ref[8 * d : 8 * d + 1, :] = c
        c = in_ref[8 * d : 8 * d + 1, :] + (c - gap_block * c)
        e = 31 - d
        out_ref[8 * e + 1 : 8 * e + 2, :] = h
        h = in_ref[8 * e + 1 : 8 * e + 2, :] + (h - gap_block * h)


def line_kernel(
    gx_ref, thick_ref, mu_ref, c32_ref, s32_ref, tc_ref, ts_ref, c128_ref, s128_ref, lam_ref,
    in_ref, out_ref,
):
    def times(a, b):
        return jnp.dot(a, b, precision=highest, preferred_element_type=f32)

    line = in_ref[pl.ds(2, 32, stride=8), :]
    ghost = in_ref[pl.ds(4, 32, stride=8), :]
    at_first = iota((32, 128), 1) == 0
    line = line + jnp.where(at_first, pltpu.roll(ghost, 1, axis=0), 0.0)
    c32, s32 = c32_ref[...], s32_ref[...]
    tc, ts = tc_ref[...], ts_ref[...]
    c128, s128 = c128_ref[...], s128_ref[...]
    re, im = times(c32, line), -times(s32, line)
    re, im = re * tc + im * ts, im * tc - re * ts
    re, im = times(re, c128) + times(im, s128), times(im, c128) - times(re, s128)
    mean = jnp.logical_and(iota((32, 128), 0) == 0, at_first)
    eigen = mu_ref[pl.ds(gx_ref[0], 1), :] + lam_ref[...]
    gain = jnp.where(mean, 0.0, (1.0 / NY) / jnp.where(mean, 1.0, eigen))
    re, im = re * gain, im * gain
    re, im = times(re, c128) - times(im, s128), times(im, c128) + times(re, s128)
    re, im = re * tc - im * ts, im * tc + re * ts
    out_ref[0:32, :] = times(c32, re) - times(s32, im)

    totals = jnp.sum(in_ref[pl.ds(3, 32, stride=8), :], axis=0, keepdims=True)
    lane = iota((1, 128), 1)
    ones = jnp.ones((1, 128), f32)
    rhs = [ones * jnp.sum(jnp.where(lane == k, totals, 0.0), axis=1, keepdims=True) for k in range(8)]
    t = [ones * thick_ref[k] for k in range(8)]
    centre = [0.5 * (t[k] + t[k + 1]) for k in range(7)]
    zero = jnp.zeros((1, 128), f32)
    upper = [1.0 / (t[k] * centre[k]) for k in range(7)] + [zero]
    lower = [zero] + [1.0 / (t[k] * centre[k - 1]) for k in range(1, 8)]
    reduced, ratio = [], []
    excess = zero
    for k in range(8):
        if k == 0:
            excess = -upper[0]
            top = rhs[0]
        else:
            excess = lower[k] * excess / (upper[k - 1] - excess)
            top = rhs[k] - lower[k] * reduced[-1]
        pivot = excess - upper[k]
        reduced.append(top / pivot)
        ratio.append(upper[k] / pivot)
    value = zero
    for k in reversed(range(8)):
        value = reduced[k] - ratio[k] * value
        out_ref[32 + k : 33 + k, :] = value * (1.0 / NX) * (1.0 / NY)


def backward_kernel(
    gx_ref, gy_ref, mu_ref, sines_ref, tc_ref, ts_ref, common_ref, first_ref, line_ref, carry_ref,
    in_ref, out_ref, p_ref, z_ref, grid_ref,
):
    eigen = eigen_table(sines_ref[...], mu_ref[pl.ds(gx_ref[0], 1), :], True)
    rho, gap, factor = decay(eigen)
    at_zero = jnp.logical_and(iota((32, 128), 0) == 0, iota((32, 128), 1) == 0)
    factor = factor * jnp.where(at_zero, 1.0 / NX, 2.0 / NX)
    south = carry_ref[pl.ds(0, 32, stride=8), :]
    north = carry_ref[pl.ds(1, 32, stride=8), :]

    def from_south(j, c):
        c = c - gap * c
        p_ref[pl.ds(j, 32, stride=ROWS), :] = in_ref[pl.ds(j, 32, stride=ROWS), :] + c
        return c

    c = lax.fori_loop(0, 128, from_south, south, unroll=8)
    c = c - gap * c
    p_ref[pl.ds(128, 32, stride=ROWS), :] = (in_ref[pl.ds(128, 32, stride=ROWS), :] + c + north) * factor

    def from_north(n, h):
        j = 127 - n
        h = h - gap * h
        p_ref[pl.ds(j, 32, stride=ROWS), :] = (p_ref[pl.ds(j, 32, stride=ROWS), :] + h) * factor
        return h

    lax.fori_loop(0, 128, from_north, north, unroll=8)
    for r in range(129, ROWS):
        p_ref[pl.ds(r, 32, stride=ROWS), :] = jnp.zeros((32, 128), f32)

    own = gy_ref[0]
    line = line_ref[pl.ds(own, 1), :] * (1.0 / NX)
    after = line_ref[pl.ds((own + 1) % 32, 1), :] * (1.0 / NX)
    lane128 = iota((128, 128), 1)
    column = jnp.where(iota((128, 128), 0) == 0, line, 0.0).T
    p_ref[0:128, :] = jnp.where(lane128 == 0, column, p_ref[0:128, :])
    lane1 = iota((1, 128), 1)
    p_ref[128:129, :] = jnp.where(lane1 == 0, after, p_ref[128:129, :])

    z_ref[0] = jnp.dot(p_ref[0:ROWS, :], first_ref[...], precision=highest, preferred_element_type=f32)

    def product(c, carry):
        start = pl.multiple_of(c * ROWS, 8)
        z_ref[c] = jnp.dot(
            p_ref[pl.ds(start, ROWS), :], common_ref[...], precision=highest, preferred_element_type=f32
        )
        return carry

    lax.fori_loop(1, 32, product, 0)

    def group(i, carry):
        start = pl.multiple_of(i * 8, 8)
        rows = pl.ds(start, 8)
        h = [(z_ref[0, rows, 0:128], z_ref[0, rows, 128:256])]
        for c in range(1, 32):
            re, im = z_ref[c, rows, 0:128], z_ref[c, rows, 128:256]
            tc, ts = tc_ref[c : c + 1, :], ts_ref[c : c + 1, :]
            h.append((re * tc - im * ts, im * tc + re * ts))
        x = backward_classes(h)
        for g in range(32):
            grid_ref[g, rows, :] = x[g]
        return carry

    lax.fori_loop(0, ROWS // 8, group, 0)

    for s in range(8):
        for part in range(4):
            tile = grid_ref[4 * s + part, 0:128, :].T
            out_ref[s, 128 * part : 128 * part + 128, :] = tile
            if part == 0 and s > 0:
                out_ref[s - 1, 512:513, :] = tile[0:1]
            out_ref[s, 513 + part : 514 + part, :] = grid_ref[4 * s + part, 128:129, :]
        out_ref[s, 517:520, :] = jnp.zeros((3, 128), f32)
    out_ref[7, 512:513, :] = jnp.zeros((1, 128), f32)


def gradient_kernel(
    gx_ref, thick_ref, unmix_ref, line_ref, p_ref, u_ref, v_ref, w_ref, uo_ref, vo_ref, wo_ref, press_ref, edge_ref
):
    step = pl.program_id(0)
    base = pl.multiple_of(step * 128, 128)
    wall = jnp.logical_and(gx_ref[0] == 7, step == 3)
    edge_ref[...] = jnp.zeros((128, 128), f32)
    for k in range(8):
        acc = p_ref[0, pl.ds(513 + step, 1), :] * unmix_ref[8 * k : 8 * k + 1, :]
        for mode in range(1, 8):
            acc = acc + p_ref[mode, pl.ds(513 + step, 1), :] * unmix_ref[8 * k + mode : 8 * k + mode + 1, :]
        edge_ref[k : k + 1, :] = acc
    edge_ref[...] = edge_ref[...].T
    for sub in range(17):
        parts = [p_ref[mode, pl.ds(base + 8 * sub, 8), :] for mode in range(8)]
        for k in range(8):
            acc = parts[0] * unmix_ref[8 * k : 8 * k + 1, :]
            for mode in range(1, 8):
                acc = acc + parts[mode] * unmix_ref[8 * k + mode : 8 * k + mode + 1, :]
            press_ref[k, 8 * sub : 8 * sub + 8, :] = acc
    lane = iota((16, 128), 1)
    row = iota((16, 128), 0)
    ones = jnp.ones((1, 128), f32)
    t = [ones * thick_ref[k] for k in range(8)]
    inverse = [2.0 / (t[k] + t[k + 1]) for k in range(7)]
    drift = [(line_ref[33 + k : 34 + k, :] - line_ref[32 + k : 33 + k, :]) * inverse[k] for k in range(7)]
    for sub in range(8):
        rows = slice(16 * sub, 16 * sub + 16)
        edge = edge_ref[rows, :]
        for k in range(8):
            p = press_ref[k, rows, :]
            east = press_ref[k, 16 * sub + 1 : 16 * sub + 17, :]
            u = u_ref[k, rows, :] - (east - p)
            if sub == 7:
                u = jnp.where(jnp.logical_and(wall, row == 15), 0.0, u)
            uo_ref[k, rows, :] = u
            north = jnp.where(lane == 127, pltpu.roll(edge, 127 - k, axis=1), pltpu.roll(p, 127, axis=1))
            vo_ref[k, rows, :] = v_ref[k, rows, :] - (north - p)
            if k < 7:
                wo_ref[k, rows, :] = w_ref[k, rows, :] - ((press_ref[k + 1, rows, :] - p) * inverse[k] + drift[k])
            else:
                wo_ref[k, rows, :] = jnp.zeros((16, 128), f32)


SMEM = pl.BlockSpec(memory_space=pltpu.SMEM)
VMEM = pl.BlockSpec(memory_space=pltpu.VMEM)


def whole(shape):
    return pl.BlockSpec(shape, lambda i: (0,) * len(shape))


def on_device(u_vel, v_vel, w_vel, thickness):
    gx = lax.axis_index("gx").astype(jnp.int32)[None]
    gy = lax.axis_index("gy").astype(jnp.int32)[None]
    common, first, tc, ts = dct_tables()
    sines = const(np.sin(math.pi * class_modes() / 8192) ** 2)
    tables = (sines, const(tc), const(ts))
    shape = jax.ShapeDtypeStruct

    mix, unmix, mu = pl.pallas_call(
        vertical_modes,
        out_shape=(shape((64, 128), f32), shape((64, 128), f32), shape((8, 128), f32)),
        in_specs=[SMEM],
        out_specs=(VMEM, VMEM, VMEM),
        name="vertical_modes",
    )(thickness)

    block = pl.BlockSpec((8, 128, 128), lambda i: (0, i, 0))
    field = (8, PAY, 128)
    packed = pl.pallas_call(
        divergence_kernel,
        out_shape=shape(field, f32),
        grid=(4,),
        in_specs=[SMEM, SMEM, whole((64, 128)), block, block, block],
        out_specs=whole(field),
        scratch_shapes=[pltpu.VMEM((64, 128), f32), pltpu.VMEM((64, 128), f32)],
        name="divergence",
    )(gx, thickness, mix, u_vel, v_vel, w_vel)
    packed = lax.all_to_all(packed, "gx", split_axis=0, concat_axis=0, tiled=True)

    local, small = pl.pallas_call(
        forward_kernel,
        out_shape=(shape((32 * ROWS, 128), f32), shape((256, 128), f32)),
        in_specs=[SMEM] + [VMEM] * 7,
        out_specs=(VMEM, VMEM),
        scratch_shapes=[
            pltpu.VMEM((32, ROWS, 128), f32),
            pltpu.VMEM((32, ROWS, 256), f32),
            pltpu.VMEM((32 * ROWS, 128), f32),
        ],
        name="forward",
    )(gx, mu, *tables, const(common), const(first), packed)
    small = lax.all_to_all(small, "gy", split_axis=0, concat_axis=0, tiled=True)

    carries = pl.pallas_call(
        carry_kernel,
        out_shape=shape((256, 128), f32),
        in_specs=[SMEM, SMEM] + [VMEM] * 3,
        out_specs=VMEM,
        name="carries",
    )(gx, gy, mu, sines, small)
    carries = lax.all_to_all(carries, "gy", split_axis=0, concat_axis=0, tiled=True)
    line = pl.pallas_call(
        line_kernel,
        out_shape=shape((40, 128), f32),
        in_specs=[SMEM, SMEM] + [VMEM] * 9,
        out_specs=VMEM,
        name="line",
    )(gx, thickness, mu, *[const(x) for x in line_tables()], small)

    packed = pl.pallas_call(
        backward_kernel,
        out_shape=shape(field, f32),
        in_specs=[SMEM, SMEM] + [VMEM] * 9,
        out_specs=VMEM,
        scratch_shapes=[
            pltpu.VMEM((32 * ROWS, 128), f32),
            pltpu.VMEM((32, ROWS, 256), f32),
            pltpu.VMEM((32, ROWS, 128), f32),
        ],
        name="backward",
    )(gx, gy, mu, *tables, const(common.T), const(first.T), line, carries, local)
    packed = lax.all_to_all(packed, "gx", split_axis=0, concat_axis=0, tiled=True)

    out = shape((8, LX, 128), f32)
    return pl.pallas_call(
        gradient_kernel,
        out_shape=(out, out, out),
        grid=(4,),
        in_specs=[SMEM, SMEM, whole((64, 128)), whole((40, 128)), whole(field), block, block, block],
        out_specs=(block, block, block),
        scratch_shapes=[pltpu.VMEM((8, 136, 128), f32), pltpu.VMEM((128, 128), f32)],
        name="gradient",
    )(gx, thickness, unmix, line, packed, u_vel, v_vel, w_vel)


def solution(mesh):
    return jax.shard_map(
        on_device,
        mesh=mesh,
        in_specs=(P(None, "gx", "gy"), P(None, "gx", "gy"), P(None, "gx", "gy"), P()),
        out_specs=(P(None, "gx", "gy"), P(None, "gx", "gy"), P(None, "gx", "gy")),
        check_vma=False,
    )
```

time: 489 us -> 158 us (0.32)
  the two profiles are of different devices: /device:TPU:41 before, /device:TPU:2 now
where the time goes in v1:
time: 158 us; the launch traced here: 157 us
  blocking collectives  63.7 us (40%)
  Pallas kernels  55.8 us (35%)
  waiting for transfers between devices  21.1 us (13%)
  starting transfers between devices  14.5 us (9%)
    all_to_all x2, blocking collectives, on_device(): lax.all_to_all(packed, 'gx', split_axis=0, concat_axis=0, tiled=True)  63.7 us
    pallas_call x1, Pallas kernels, on_device(): pl.pallas_call(forward_kernel, out_shape=(shape((32 * ROWS, 128), f32), s...  16.1 us
    pallas_call x1, Pallas kernels, on_device(): pl.pallas_call(backward_kernel, out_shape=shape(field, f32), in_specs=[SM...  15.9 us
    all_to_all x1, waiting for transfers between devices, on_device(): small = lax.all_to_all(small, 'gy', split_axis=0, concat_axis=0, tiled=True)  11.9 us
    all_to_all x1, starting transfers between devices, on_device(): small = lax.all_to_all(small, 'gy', split_axis=0, concat_axis=0, tiled=True)  10.7 us
    all_to_all x1, waiting for transfers between devices, on_device(): lax.all_to_all(carries, 'gy', split_axis=0, concat_axis=0, tiled=True)  9.21 us
    pallas_call x1, Pallas kernels, on_device(): pl.pallas_call(gradient_kernel, out_shape=(out, out, out), grid=(4,), in_...  7.94 us
    pallas_call x1, Pallas kernels, on_device(): pl.pallas_call(divergence_kernel, out_shape=shape(field, f32), grid=(4,),...  6.28 us
  transfers between devices with their start and end apart: 2, of which 2 were waited for; matrix products, arithmetic and copies ran while one was open for 0% of the time, Pallas kernels for 2%

profile of v1, /device:TPU:2, one launch (start us, length us, event | category | flops | bytes accessed | tf_op | source)
XLA Modules:
  0.0 157.2 jit_solution(721089805990637935)
XLA Ops:
  0.6 5.0 %vertical_modes.1 = (f32[64,128]{1,0:T(8,128)}, f32[64,128]{1,0:T(8,128)}, f32[8,128]{1,0:T(8,128)}) custom-call(f32[8]{0:T(128)} %thick_ref.7), custom_call_target="tpu_custom_call" | custom-call | tf_op jit(solution)/shard_map/vertical_modes/pallas_call | solution.py:633
  5.6 6.3 %divergence.1 = f32[8,520,128]{2,1,0:T(8,128)} custom-call(s32[1]{0:T(128)} %bitcast.gx_ref, f32[8]{0:T(128)} %thick_ref.7, f32[64,128]{1,0:T(8,128)} %get-tuple-element.10.mix_ref, f32[8,512,128]{2,1,0:T(8,128)} %u_ref.3, f32[8,512,128]{2,1,0:T(8,128)} %v_ref.3, f32[8,512,128]{2,1,0:T(8,128)} %w_ref.3), custom_call_target="tpu_custom_call" | custom-call | tf_op jit(solution)/shard_map/divergence/pallas_call | solution.py:643
  11.9 32.1 %all_to_all.32.in_ref = f32[8,520,128]{2,1,0:T(8,128)} all-to-all(f32[8,520,128]{2,1,0:T(8,128)} %divergence.1), channel_id=1, replica_groups=mesh['gx'=8,'gy'=32] {'gx'}, dimensions={0} | all-to-all | bytes 4259840 | tf_op jit(solution)/shard_map/all_to_all | solution.py:652
  44.1 16.1 %forward.1 = (f32[4352,128]{1,0:T(8,128)}, f32[256,128]{1,0:T(8,128)}) custom-call(s32[1]{0:T(128)} %bitcast.gx_ref, f32[8,128]{1,0:T(8,128)} %get-tuple-element.9.mu_ref, f32[32,128]{1,0:T(8,128)} %constant.37.clone.sines_ref, f32[32,128]{1,0:T(8,128)} %constant.38.clone.tc_ref, f32[32,128]{1,0:T(8,128)} %constant.39.clone.ts_ref, ...), custom_call_target="tpu_custom_call" | custom-call | tf_op jit(solution)/shard_map/forward/pallas_call | solution.py:654
  60.2 10.7 %all-to-all-start.1 = ((f32[32,8,128]{2,1,0:T(8,128)}), f32[32,8,128]{2,1,0:T(8,128)S(1)}, u32[]{:S(2)}, u32[]{:S(2)}) async-start(f32[32,8,128]{2,1,0:T(8,128)} %bitcast.10), calls=%async_computation.1 | async-start | bytes 262144 | tf_op jit(solution)/shard_map/all_to_all | solution.py:666
  70.9 11.9 %all-to-all-done.1 = f32[32,8,128]{2,1,0:T(8,128)S(1)} async-done(((f32[32,8,128]{2,1,0:T(8,128)}), f32[32,8,128]{2,1,0:T(8,128)S(1)}, u32[]{:S(2)}, u32[]{:S(2)}) %all-to-all-start.1) | async-done | bytes 131104 | tf_op jit(solution)/shard_map/all_to_all | solution.py:666
  82.8 0.0 copy-start
  82.8 0.7 copy-done
  83.5 1.8 %carries.1 = f32[256,128]{1,0:T(8,128)} custom-call(s32[1]{0:T(128)} %bitcast.gx_ref, s32[1]{0:T(128)} %bitcast.3.gy_ref, f32[8,128]{1,0:T(8,128)} %get-tuple-element.9.mu_ref, f32[32,128]{1,0:T(8,128)} %constant.37.clone.sines_ref, f32[256,128]{1,0:T(8,128)} %bitcast.6), custom_call_target="tpu_custom_call" | custom-call | tf_op jit(solution)/shard_map/carries/pallas_call | solution.py:668
  85.3 3.9 %all-to-all-start.2 = ((f32[32,8,128]{2,1,0:T(8,128)}), f32[32,8,128]{2,1,0:T(8,128)S(1)}, u32[]{:S(2)}, u32[]{:S(2)}) async-start(f32[32,8,128]{2,1,0:T(8,128)} %bitcast.8), calls=%async_computation.2 | async-start | bytes 262144 | tf_op jit(solution)/shard_map/all_to_all | solution.py:675
  89.2 2.7 %line.1.line_ref = f32[40,128]{1,0:T(8,128)} custom-call(s32[1]{0:T(128)} %bitcast.gx_ref, f32[8]{0:T(128)} %thick_ref.7, f32[8,128]{1,0:T(8,128)} %get-tuple-element.9.mu_ref, f32[32,32]{1,0:T(8,128)} %constant.42.clone.c32_ref, f32[32,32]{1,0:T(8,128)} %constant.43.clone.s32_ref, f32[32,128]{1,0:T(8,128)} %constant.44.clone.tc_ref, ...), custom_call_target="tpu_custom_call" | custom-call | tf_op jit(solution)/shard_map/line/pallas_call | solution.py:676
  91.9 9.2 %all-to-all-done.2 = f32[32,8,128]{2,1,0:T(8,128)S(1)} async-done(((f32[32,8,128]{2,1,0:T(8,128)}), f32[32,8,128]{2,1,0:T(8,128)S(1)}, u32[]{:S(2)}, u32[]{:S(2)}) %all-to-all-start.2) | async-done | bytes 131104 | tf_op jit(solution)/shard_map/all_to_all | solution.py:675
  101.1 0.0 copy-start.1
  101.1 0.7 copy-done.1
  101.7 15.9 %backward.1 = f32[8,520,128]{2,1,0:T(8,128)} custom-call(s32[1]{0:T(128)} %bitcast.gx_ref, s32[1]{0:T(128)} %bitcast.3.gy_ref, f32[8,128]{1,0:T(8,128)} %get-tuple-element.9.mu_ref, f32[32,128]{1,0:T(8,128)} %constant.37.clone.sines_ref, f32[32,128]{1,0:T(8,128)} %constant.38.clone.tc_ref, f32[32,128]{1,0:T(8,128)} %constant.39.clone.ts_ref, ...), custom_call_target="tpu_custom_call" | custom-call | tf_op jit(solution)/shard_map/backward/pallas_call | solution.py:684
  117.7 31.5 %all_to_all.33.p_ref = f32[8,520,128]{2,1,0:T(8,128)} all-to-all(f32[8,520,128]{2,1,0:T(8,128)} %backward.1), channel_id=1, replica_groups=mesh['gx'=8,'gy'=32] {'gx'}, dimensions={0} | all-to-all | bytes 4259840 | tf_op jit(solution)/shard_map/all_to_all | solution.py:696
  149.2 7.9 %gradient.1 = (f32[8,512,128]{2,1,0:T(8,128)}, f32[8,512,128]{2,1,0:T(8,128)}, f32[8,512,128]{2,1,0:T(8,128)}) custom-call(s32[1]{0:T(128)} %bitcast.gx_ref, f32[8]{0:T(128)} %thick_ref.7, f32[64,128]{1,0:T(8,128)} %get-tuple-element.8.unmix_ref, f32[40,128]{1,0:T(8,128)} %line.1.line_ref, f32[8,520,128]{2,1,0:T(8,128)} %all_to_all.33.p_ref, ...), custom_call_target="tpu_custom_call" | custom-call | tf_op jit(solution)/shard_map/gradient/pallas_call | solution.py:699
Async XLA Ops:
  60.2 22.6 %all-to-all-start.1 = ((f32[32,8,128]{2,1,0:T(8,128)}), f32[32,8,128]{2,1,0:T(8,128)S(1)}, u32[]{:S(2)}, u32[]{:S(2)}) async-start(f32[32,8,128]{2,1,0:T(8,128)} %bitcast.10), calls=%async_computation.1 | async-start | bytes 262144 | tf_op jit(solution)/shard_map/all_to_all | solution.py:666
  82.8 0.7 copy-start
  85.3 15.8 %all-to-all-start.2 = ((f32[32,8,128]{2,1,0:T(8,128)}), f32[32,8,128]{2,1,0:T(8,128)S(1)}, u32[]{:S(2)}, u32[]{:S(2)}) async-start(f32[32,8,128]{2,1,0:T(8,128)} %bitcast.8), calls=%async_computation.2 | async-start | bytes 262144 | tf_op jit(solution)/shard_map/all_to_all | solution.py:675
  101.1 0.7 copy-start.1

commit v2 on v1

--- a/solution.py
+++ b/solution.py
@@ -15,6 +15,7 @@
 NZ = 8
 LX = 512
 ROWS = 136
+BATCH = 4
 PAY = 520
 HALF = float(np.sqrt(0.5))
 
@@ -52,6 +53,61 @@
     q = d[:, None] + 32 * j[None, :]
     lam = -4.0 * np.sin(math.pi * q / NY) ** 2
     return np.cos(a32), np.sin(a32), np.cos(tw), np.sin(tw), np.cos(a128), np.sin(a128), lam
+
+
+def three_parts(values):
+    rest = np.asarray(values, dtype=np.float32)
+    parts = []
+    for _ in range(3):
+        part = rest.astype(jnp.bfloat16)
+        parts.append(part)
+        rest = rest - part.astype(np.float32)
+    return parts
+
+
+def forward_weights(matrix):
+    high, mid, low = three_parts(matrix)
+    return jnp.asarray(np.concatenate([high, mid, low, np.zeros_like(low)], axis=1))
+
+
+def backward_weights(matrix):
+    high, mid, low = three_parts(matrix.T)
+    return jnp.asarray(np.concatenate([high, high, mid, mid, low, high], axis=0))
+
+
+def head(x):
+    scaled = x * 65537.0
+    return scaled - (scaled - x)
+
+
+def split(x):
+    high = x.astype(jnp.bfloat16)
+    rest = x - high.astype(f32)
+    mid = head(rest)
+    return high, mid.astype(jnp.bfloat16), (rest - mid).astype(jnp.bfloat16)
+
+
+def times_bf16(a, b):
+    return jnp.dot(a, b, preferred_element_type=f32)
+
+
+def forward_product(x, w_ref):
+    high, mid, low = split(x)
+    both = times_bf16(high, w_ref[:, 0:256]) + times_bf16(mid, w_ref[:, 0:256])
+    rest = times_bf16(high, w_ref[:, 256:384]) + times_bf16(low, w_ref[:, 0:128])
+    return both[:, 0:128] + (both[:, 128:256] + rest)
+
+
+def backward_product(x, w_ref):
+    high, mid, low = split(x)
+    two = jnp.concatenate([high, mid], axis=1)
+    rest = times_bf16(two, w_ref[256:512, :]) + times_bf16(jnp.concatenate([high, low], axis=1), w_ref[512:768, :])
+    return times_bf16(two, w_ref[0:256, :]) + rest
+
+
+def slow_table():
+    slow = class_modes()[:, [0, 1, 2, 3, 64, 65, 66, 67]].T
+    return np.sin(math.pi * np.tile(slow, (1, 4)) / 8192) ** 2
 
 
 def const(values):
@@ -264,74 +320,89 @@
     return lax.broadcasted_iota(jnp.int32, shape, axis)
 
 
-def divergence_kernel(gx_ref, thick_ref, mix_ref, u_ref, v_ref, w_ref, out_ref, last_ref, sum_ref):
-    step = pl.program_id(0)
-    wall = jnp.logical_and(gx_ref[0] == 7, step == 3)
-
-    @pl.when(step == 0)
-    def _():
-        last_ref[...] = jnp.zeros((64, 128), f32)
-        sum_ref[...] = jnp.zeros((64, 128), f32)
-
+def divergence_kernel(
+    gx_ref, thick_ref, u_hbm, v_hbm, w_hbm, out_ref, unmix_ref, mu_ref,
+    mix_ref, u_ref, v_ref, w_ref, last_ref, sum_ref, sems,
+):
+    def copies(step):
+        rows = pl.ds(128 * step, 128)
+        return [
+            pltpu.make_async_copy(src.at[:, rows, :], dst.at[:, rows, :], sems.at[n, step])
+            for n, (src, dst) in enumerate(((u_hbm, u_ref), (v_hbm, v_ref), (w_hbm, w_ref)))
+        ]
+
+    for step in range(4):
+        for copy in copies(step):
+            copy.start()
+    vertical_modes(thick_ref, mix_ref, unmix_ref, mu_ref)
+
+    last_ref[...] = jnp.zeros((64, 128), f32)
+    sum_ref[...] = jnp.zeros((64, 128), f32)
     lane = iota((16, 128), 1)
     row = iota((16, 128), 0)
+    lanes = iota((128, 128), 1)
     ones = jnp.ones((1, 128), f32)
     inverse = [1.0 / (ones * thick_ref[k]) for k in range(8)]
-    base = pl.multiple_of(step * 128, 128)
-    for sub in range(8):
-        rows = slice(16 * sub, 16 * sub + 16)
-        div = []
-        below = None
+
+    def block(step, carry):
+        for copy in copies(step):
+            copy.wait()
+        wall = jnp.logical_and(gx_ref[0] == 7, step == 3)
+        base = pl.multiple_of(step * 128, 128)
+        for sub in range(8):
+            rows = pl.ds(base + 16 * sub, 16)
+            div = []
+            below = None
+            for k in range(8):
+                u = u_ref[k, rows, :]
+                if sub == 7:
+                    u = jnp.where(jnp.logical_and(wall, row == 15), 0.0, u)
+                prev = pltpu.roll(u, 1, axis=0)
+                prev = jnp.where(row == 0, last_ref[8 * k : 8 * k + 1, :], prev)
+                last_ref[8 * k : 8 * k + 1, :] = u[15:16]
+                v = v_ref[k, rows, :]
+                back = jnp.where(lane == 0, 0.0, pltpu.roll(v, 1, axis=1))
+                if k < 7:
+                    w = w_ref[k, rows, :]
+                    up = w if below is None else w - below
+                    below = w
+                else:
+                    up = -below
+                rise = up * inverse[k]
+                sum_ref[8 * k : 8 * k + 8, :] += rise[0:8] + rise[8:16]
+                div.append((u - prev) + (v - back) + rise)
+            for mode in range(8):
+                acc = div[0] * mix_ref[8 * mode : 8 * mode + 1, :]
+                for k in range(1, 8):
+                    acc = acc + div[k] * mix_ref[8 * mode + k : 8 * mode + k + 1, :]
+                out_ref[mode, rows, :] = acc
+
+        edge = jnp.zeros((128, 128), f32)
         for k in range(8):
-            u = u_ref[k, rows, :]
-            if sub == 7:
-                u = jnp.where(jnp.logical_and(wall, row == 15), 0.0, u)
-            prev = pltpu.roll(u, 1, axis=0)
-            prev = jnp.where(row == 0, last_ref[8 * k : 8 * k + 1, :], prev)
-            last_ref[8 * k : 8 * k + 1, :] = u[15:16]
-            v = v_ref[k, rows, :]
-            back = jnp.where(lane == 0, 0.0, pltpu.roll(v, 1, axis=1))
-            if k < 7:
-                w = w_ref[k, rows, :]
-                up = w if below is None else w - below
-                below = w
-            else:
-                up = -below
-            rise = up * inverse[k]
-            sum_ref[8 * k : 8 * k + 8, :] += rise[0:8] + rise[8:16]
-            div.append((u - prev) + (v - back) + rise)
+            edge = jnp.where(lanes == k, pltpu.roll(v_ref[k, pl.ds(base, 128), :], k + 1, axis=1), edge)
+        edge = edge.T
         for mode in range(8):
-            acc = div[0] * mix_ref[8 * mode : 8 * mode + 1, :]
+            acc = edge[0:1] * mix_ref[8 * mode : 8 * mode + 1, :]
             for k in range(1, 8):
-                acc = acc + div[k] * mix_ref[8 * mode + k : 8 * mode + k + 1, :]
-            out_ref[mode, pl.ds(base + 16 * sub, 16), :] = acc
-
-    lanes = iota((128, 128), 1)
-    edge = jnp.zeros((128, 128), f32)
+                acc = acc + edge[k : k + 1] * mix_ref[8 * mode + k : 8 * mode + k + 1, :]
+            out_ref[mode, pl.ds(513 + step, 1), :] = -acc
+        return carry
+
+    lax.fori_loop(0, 4, block, 0)
+
+    lane1 = iota((1, 128), 1)
+    totals = jnp.zeros((1, 128), f32)
     for k in range(8):
-        edge = jnp.where(lanes == k, pltpu.roll(v_ref[k], k + 1, axis=1), edge)
-    edge = edge.T
+        part = jnp.sum(sum_ref[8 * k : 8 * k + 8, :], axis=0, keepdims=True)
+        part = jnp.sum(part, axis=1, keepdims=True)
+        totals = jnp.where(lane1 == k, part, totals)
     for mode in range(8):
-        acc = edge[0:1] * mix_ref[8 * mode : 8 * mode + 1, :]
+        acc = last_ref[0:1, :] * mix_ref[8 * mode : 8 * mode + 1, :]
         for k in range(1, 8):
-            acc = acc + edge[k : k + 1] * mix_ref[8 * mode + k : 8 * mode + k + 1, :]
-        out_ref[mode, pl.ds(513 + step, 1), :] = -acc
-
-    @pl.when(step == 3)
-    def _():
-        lane1 = iota((1, 128), 1)
-        totals = jnp.zeros((1, 128), f32)
-        for k in range(8):
-            part = jnp.sum(sum_ref[8 * k : 8 * k + 8, :], axis=0, keepdims=True)
-            part = jnp.sum(part, axis=1, keepdims=True)
-            totals = jnp.where(lane1 == k, part, totals)
-        for mode in range(8):
-            acc = last_ref[0:1, :] * mix_ref[8 * mode : 8 * mode + 1, :]
-            for k in range(1, 8):
-                acc = acc + last_ref[8 * k : 8 * k + 1, :] * mix_ref[8 * mode + k : 8 * mode + k + 1, :]
-            out_ref[mode, 512:513, :] = acc
-            out_ref[mode, 517:518, :] = totals
-            out_ref[mode, 518:520, :] = jnp.zeros((2, 128), f32)
+            acc = acc + last_ref[8 * k : 8 * k + 1, :] * mix_ref[8 * mode + k : 8 * mode + k + 1, :]
+        out_ref[mode, 512:513, :] = acc
+        out_ref[mode, 517:518, :] = totals
+        out_ref[mode, 518:520, :] = jnp.zeros((2, 128), f32)
 
 
 def eigen_table(sines, mu_row, with_first):
@@ -344,7 +415,7 @@
 
 def forward_kernel(
     gx_ref, mu_ref, sines_ref, tc_ref, ts_ref, common_ref, first_ref, in_ref, out_ref, small_ref,
-    grid_ref, y_ref, side_ref,
+    south_ref, north_ref, grid_ref, y_ref, side_ref, turn_ref,
 ):
     row8 = iota((8, 128), 0)
     row128 = iota((128, 128), 0)
@@ -359,29 +430,30 @@
 
     def group(i, carry):
         start = pl.multiple_of(i * 8, 8)
-        rows = pl.ds(start, 8)
-        y = forward_classes([grid_ref[g, rows, :] for g in range(32)])
-        y_ref[0, rows, 0:128] = y[0][0]
-        y_ref[0, rows, 128:256] = y[0][1]
+        y = forward_classes([grid_ref[g, pl.ds(start, 8), :] for g in range(32)])
+        y_ref[pl.ds(start, 8), 0:128] = y[0][0]
+        y_ref[pl.ds(start, 8), 128:256] = y[0][1]
         for c in range(1, 32):
             re, im = y[c]
             tc, ts = tc_ref[c : c + 1, :], ts_ref[c : c + 1, :]
-            y_ref[c, rows, 0:128] = re * tc + im * ts
-            y_ref[c, rows, 128:256] = im * tc - re * ts
+            rows = pl.ds(start + ROWS * c, 8)
+            y_ref[rows, 0:128] = re * tc + im * ts
+            y_ref[rows, 128:256] = im * tc - re * ts
         return carry
 
     lax.fori_loop(0, ROWS // 8, group, 0)
 
-    out_ref[0:ROWS, :] = jnp.dot(y_ref[0], first_ref[...], precision=highest, preferred_element_type=f32)
-
-    def product(c, carry):
-        start = pl.multiple_of(c * ROWS, 8)
-        out_ref[pl.ds(start, ROWS), :] = jnp.dot(
-            y_ref[c], common_ref[...], precision=highest, preferred_element_type=f32
-        )
+    batch = BATCH * ROWS
+
+    def product(n, carry):
+        start = pl.multiple_of(n * batch, 8)
+        out_ref[pl.ds(start, batch), :] = forward_product(y_ref[pl.ds(start, batch), :], common_ref)
         return carry
 
-    lax.fori_loop(1, 32, product, 0)
+    lax.fori_loop(0, 32 // BATCH, product, 0)
+    out_ref[0:144, :] = jnp.where(
+        iota((144, 128), 0) < ROWS, forward_product(y_ref[0:144, :], first_ref), out_ref[0:144, :]
+    )
 
     line = out_ref[0:128, :].T[0:1]
     ghost_line = out_ref[128:129, :]
@@ -408,49 +480,54 @@
     totals = in_ref[0, 517:518, :]
     for s in range(1, 8):
         totals = totals + in_ref[s, 517:518, :]
-    small_ref[pl.ds(0, 32, stride=8), :] = f + ghost / rho
-    small_ref[pl.ds(1, 32, stride=8), :] = b
-    small_ref[pl.ds(2, 32, stride=8), :] = jnp.broadcast_to(line, (32, 128))
-    small_ref[pl.ds(3, 32, stride=8), :] = jnp.broadcast_to(totals, (32, 128))
-    small_ref[pl.ds(4, 32, stride=8), :] = jnp.broadcast_to(ghost_line, (32, 128))
-    for r in (5, 6, 7):
-        small_ref[pl.ds(r, 32, stride=8), :] = jnp.zeros((32, 128), f32)
-
-
-def carry_kernel(gx_ref, gy_ref, mu_ref, sines_ref, in_ref, out_ref):
-    own = gy_ref[0]
-    eigen = mu_ref[pl.ds(gx_ref[0], 1), :] - 4.0 * sines_ref[pl.ds(own, 1), :]
-    first = jnp.logical_and(own == 0, iota((1, 128), 1) == 0)
-    eigen = jnp.where(first, -1.0, eigen)
-    _, gap, _ = decay(eigen)
-    gap_block = doubled(gap, 7)
-    around = 1.0 / doubled(gap_block, 5)
-    c = jnp.zeros((1, 128), f32)
-    h = jnp.zeros((1, 128), f32)
+    f = f + ghost / rho
+    south_ref[...] = f
+    north_ref[...] = b
+    turn_ref[0:32, :] = f
+    turn_ref[32:64, :] = b
+    turn_ref[64:128, :] = jnp.zeros((64, 128), f32)
+    turn_ref[...] = turn_ref[...].T
+    turn_ref[4:8, :] = turn_ref[64:68, :]
+    lane1 = iota((1, 128), 1)
+    extra = [pltpu.roll(line, 64, axis=1), line, pltpu.roll(totals, 64, axis=1), pltpu.roll(ghost_line, 64, axis=1)]
+    for r in range(4):
+        turn_ref[r : r + 1, :] = jnp.where(lane1 < 64, turn_ref[r : r + 1, :], extra[r])
     for d in range(32):
-        c = in_ref[8 * d : 8 * d + 1, :] + (c - gap_block * c)
-        e = 31 - d
-        h = in_ref[8 * e + 1 : 8 * e + 2, :] + (h - gap_block * h)
-    c = c * around
-    h = h * around
-    out_ref[...] = jnp.zeros((256, 128), f32)
-    for d in range(32):
-        out_ref[8 * d : 8 * d + 1, :] = c
-        c = in_ref[8 * d : 8 * d + 1, :] + (c - gap_block * c)
-        e = 31 - d
-        out_ref[8 * e + 1 : 8 * e + 2, :] = h
-        h = in_ref[8 * e + 1 : 8 * e + 2, :] + (h - gap_block * h)
+        small_ref[8 * d : 8 * d + 8, :] = turn_ref[0:8, :]
 
 
 def line_kernel(
-    gx_ref, thick_ref, mu_ref, c32_ref, s32_ref, tc_ref, ts_ref, c128_ref, s128_ref, lam_ref,
-    in_ref, out_ref,
+    gx_ref, gy_ref, thick_ref, mu_ref, slow_ref, c32_ref, s32_ref, tc_ref, ts_ref, c128_ref, s128_ref, lam_ref,
+    in_ref, out_ref, turn_ref,
 ):
     def times(a, b):
         return jnp.dot(a, b, precision=highest, preferred_element_type=f32)
 
-    line = in_ref[pl.ds(2, 32, stride=8), :]
-    ghost = in_ref[pl.ds(4, 32, stride=8), :]
+    own = gy_ref[0]
+    eigen = mu_ref[pl.ds(gx_ref[0], 1), :] - 4.0 * slow_ref[...]
+    lane8 = iota((8, 128), 1)
+    first = jnp.logical_and(iota((8, 128), 0) == 0, lane8 % 32 == 0)
+    _, gap, _ = decay(jnp.where(first, -1.0, eigen))
+    gap_block = doubled(gap, 7)
+    around = 1.0 / doubled(gap_block, 5)
+    c = jnp.zeros((8, 128), f32)
+    h = jnp.zeros((8, 128), f32)
+    for e in range(32, 0, -1):
+        c = in_ref[pl.ds(pl.multiple_of((own + 32 - e) % 32 * 8, 8), 8), :] + (c - gap_block * c)
+        h = in_ref[pl.ds(pl.multiple_of((own + e) % 32 * 8, 8), 8), :] + (h - gap_block * h)
+    carry = jnp.where(lane8 < 32, c, h) * around
+    turn_ref[...] = jnp.zeros((128, 128), f32)
+    turn_ref[0:4, :] = carry[0:4]
+    turn_ref[64:68, :] = carry[4:8]
+    out_ref[40:104, :] = turn_ref[...].T[0:64]
+
+    lane32 = iota((32, 128), 1)
+    line = jnp.where(
+        lane32 < 64,
+        pltpu.roll(in_ref[pl.ds(0, 32, stride=8), :], 64, axis=1),
+        in_ref[pl.ds(1, 32, stride=8), :],
+    )
+    ghost = pltpu.roll(in_ref[pl.ds(3, 32, stride=8), :], 64, axis=1)
     at_first = iota((32, 128), 1) == 0
     line = line + jnp.where(at_first, pltpu.roll(ghost, 1, axis=0), 0.0)
     c32, s32 = c32_ref[...], s32_ref[...]
@@ -467,7 +544,8 @@
     re, im = re * tc - im * ts, im * tc + re * ts
     out_ref[0:32, :] = times(c32, re) - times(s32, im)
 
-    totals = jnp.sum(in_ref[pl.ds(3, 32, stride=8), :], axis=0, keepdims=True)
+    totals = jnp.sum(in_ref[pl.ds(2, 32, stride=8), :], axis=0, keepdims=True)
+    totals = pltpu.roll(totals, 64, axis=1)
     lane = iota((1, 128), 1)
     ones = jnp.ones((1, 128), f32)
     rhs = [ones * jnp.sum(jnp.where(lane == k, totals, 0.0), axis=1, keepdims=True) for k in range(8)]
@@ -495,15 +573,16 @@
 
 
 def backward_kernel(
-    gx_ref, gy_ref, mu_ref, sines_ref, tc_ref, ts_ref, common_ref, first_ref, line_ref, carry_ref,
-    in_ref, out_ref, p_ref, z_ref, grid_ref,
+    gx_ref, gy_ref, mu_ref, sines_ref, tc_ref, ts_ref, common_ref, first_ref, line_ref, south_ref,
+    north_ref, in_ref, out_ref, p_ref, z_ref, grid_ref,
 ):
     eigen = eigen_table(sines_ref[...], mu_ref[pl.ds(gx_ref[0], 1), :], True)
     rho, gap, factor = decay(eigen)
     at_zero = jnp.logical_and(iota((32, 128), 0) == 0, iota((32, 128), 1) == 0)
     factor = factor * jnp.where(at_zero, 1.0 / NX, 2.0 / NX)
-    south = carry_ref[pl.ds(0, 32, stride=8), :]
-    north = carry_ref[pl.ds(1, 32, stride=8), :]
+    slow = iota((32, 128), 1) % 64 < 4
+    south = jnp.where(slow, line_ref[40:72, :], south_ref[...])
+    north = jnp.where(slow, line_ref[72:104, :], north_ref[...])
 
     def from_south(j, c):
         c = c - gap * c
@@ -533,23 +612,23 @@
     lane1 = iota((1, 128), 1)
     p_ref[128:129, :] = jnp.where(lane1 == 0, after, p_ref[128:129, :])
 
-    z_ref[0] = jnp.dot(p_ref[0:ROWS, :], first_ref[...], precision=highest, preferred_element_type=f32)
-
-    def product(c, carry):
-        start = pl.multiple_of(c * ROWS, 8)
-        z_ref[c] = jnp.dot(
-            p_ref[pl.ds(start, ROWS), :], common_ref[...], precision=highest, preferred_element_type=f32
-        )
+    batch = BATCH * ROWS
+
+    def product(n, carry):
+        start = pl.multiple_of(n * batch, 8)
+        z_ref[pl.ds(start, batch), :] = backward_product(p_ref[pl.ds(start, batch), :], common_ref)
         return carry
 
-    lax.fori_loop(1, 32, product, 0)
+    lax.fori_loop(0, 32 // BATCH, product, 0)
+    z_ref[0:ROWS, :] = backward_product(p_ref[0:144, :], first_ref)[0:ROWS]
 
     def group(i, carry):
         start = pl.multiple_of(i * 8, 8)
         rows = pl.ds(start, 8)
-        h = [(z_ref[0, rows, 0:128], z_ref[0, rows, 128:256])]
+        h = [(z_ref[rows, 0:128], z_ref[rows, 128:256])]
         for c in range(1, 32):
-            re, im = z_ref[c, rows, 0:128], z_ref[c, rows, 128:256]
+            part = pl.ds(start + ROWS * c, 8)
+            re, im = z_ref[part, 0:128], z_ref[part, 128:256]
             tc, ts = tc_ref[c : c + 1, :], ts_ref[c : c + 1, :]
             h.append((re * tc - im * ts, im * tc + re * ts))
         x = backward_classes(h)
@@ -618,6 +697,10 @@
 VMEM = pl.BlockSpec(memory_space=pltpu.VMEM)
 
 
+def params(mib):
+    return pltpu.CompilerParams(vmem_limit_bytes=mib * 2**20)
+
+
 def whole(shape):
     return pl.BlockSpec(shape, lambda i: (0,) * len(shape))
 
@@ -630,69 +713,71 @@
     tables = (sines, const(tc), const(ts))
     shape = jax.ShapeDtypeStruct
 
-    mix, unmix, mu = pl.pallas_call(
-        vertical_modes,
-        out_shape=(shape((64, 128), f32), shape((64, 128), f32), shape((8, 128), f32)),
-        in_specs=[SMEM],
-        out_specs=(VMEM, VMEM, VMEM),
-        name="vertical_modes",
-    )(thickness)
-
     block = pl.BlockSpec((8, 128, 128), lambda i: (0, i, 0))
     field = (8, PAY, 128)
-    packed = pl.pallas_call(
+    local_field = pltpu.VMEM((8, LX, 128), f32)
+    packed, unmix, mu = pl.pallas_call(
         divergence_kernel,
-        out_shape=shape(field, f32),
-        grid=(4,),
-        in_specs=[SMEM, SMEM, whole((64, 128)), block, block, block],
-        out_specs=whole(field),
-        scratch_shapes=[pltpu.VMEM((64, 128), f32), pltpu.VMEM((64, 128), f32)],
+        out_shape=(shape(field, f32), shape((64, 128), f32), shape((8, 128), f32)),
+        in_specs=[SMEM, SMEM] + [pl.BlockSpec(memory_space=pltpu.HBM)] * 3,
+        out_specs=(VMEM, VMEM, VMEM),
+        scratch_shapes=[
+            pltpu.VMEM((64, 128), f32),
+            local_field,
+            local_field,
+            local_field,
+            pltpu.VMEM((64, 128), f32),
+            pltpu.VMEM((64, 128), f32),
+            pltpu.SemaphoreType.DMA((3, 4)),
+        ],
+        compiler_params=params(12),
         name="divergence",
-    )(gx, thickness, mix, u_vel, v_vel, w_vel)
+    )(gx, thickness, u_vel, v_vel, w_vel)
     packed = lax.all_to_all(packed, "gx", split_axis=0, concat_axis=0, tiled=True)
 
-    local, small = pl.pallas_call(
+    rows = shape((32, 128), f32)
+    local, small, south, north = pl.pallas_call(
         forward_kernel,
-        out_shape=(shape((32 * ROWS, 128), f32), shape((256, 128), f32)),
+        out_shape=(shape((32 * ROWS, 128), f32), shape((256, 128), f32), rows, rows),
         in_specs=[SMEM] + [VMEM] * 7,
-        out_specs=(VMEM, VMEM),
+        out_specs=(VMEM, VMEM, VMEM, VMEM),
         scratch_shapes=[
             pltpu.VMEM((32, ROWS, 128), f32),
-            pltpu.VMEM((32, ROWS, 256), f32),
+            pltpu.VMEM((32 * ROWS, 256), f32),
             pltpu.VMEM((32 * ROWS, 128), f32),
+            pltpu.VMEM((128, 128), f32),
         ],
+        compiler_params=params(20),
         name="forward",
-    )(gx, mu, *tables, const(common), const(first), packed)
+    )(gx, mu, *tables, forward_weights(common), forward_weights(first), packed)
     small = lax.all_to_all(small, "gy", split_axis=0, concat_axis=0, tiled=True)
 
-    carries = pl.pallas_call(
-        carry_kernel,
-        out_shape=shape((256, 128), f32),
-        in_specs=[SMEM, SMEM] + [VMEM] * 3,
-        out_specs=VMEM,
-        name="carries",
-    )(gx, gy, mu, sines, small)
-    carries = lax.all_to_all(carries, "gy", split_axis=0, concat_axis=0, tiled=True)
+    parts = lax.axis_size("gy")
+    south = lax.ppermute(south, "gy", [(i, (i + 1) % parts) for i in range(parts)])
+    north = lax.ppermute(north, "gy", [(i, (i - 1) % parts) for i in range(parts)])
     line = pl.pallas_call(
         line_kernel,
-        out_shape=shape((40, 128), f32),
-        in_specs=[SMEM, SMEM] + [VMEM] * 9,
+        out_shape=shape((104, 128), f32),
+        in_specs=[SMEM, SMEM, SMEM] + [VMEM] * 10,
         out_specs=VMEM,
+        scratch_shapes=[pltpu.VMEM((128, 128), f32)],
+        compiler_params=params(4),
         name="line",
-    )(gx, thickness, mu, *[const(x) for x in line_tables()], small)
+    )(gx, gy, thickness, mu, const(slow_table()), *[const(x) for x in line_tables()], small)
 
     packed = pl.pallas_call(
         backward_kernel,
         out_shape=shape(field, f32),
-        in_specs=[SMEM, SMEM] + [VMEM] * 9,
+        in_specs=[SMEM, SMEM] + [VMEM] * 10,
         out_specs=VMEM,
+        compiler_params=params(20),
         scratch_shapes=[
             pltpu.VMEM((32 * ROWS, 128), f32),
-            pltpu.VMEM((32, ROWS, 256), f32),
+            pltpu.VMEM((32 * ROWS, 256), f32),
             pltpu.VMEM((32, ROWS, 128), f32),
         ],
         name="backward",
-    )(gx, gy, mu, *tables, const(common.T), const(first.T), line, carries, local)
+    )(gx, gy, mu, *tables, backward_weights(common), backward_weights(first), line, south, north, local)
     packed = lax.all_to_all(packed, "gx", split_axis=0, concat_axis=0, tiled=True)
 
     out = shape((8, LX, 128), f32)
@@ -700,9 +785,10 @@
         gradient_kernel,
         out_shape=(out, out, out),
         grid=(4,),
-        in_specs=[SMEM, SMEM, whole((64, 128)), whole((40, 128)), whole(field), block, block, block],
+        in_specs=[SMEM, SMEM, whole((64, 128)), whole((104, 128)), whole(field), block, block, block],
         out_specs=(block, block, block),
         scratch_shapes=[pltpu.VMEM((8, 136, 128), f32), pltpu.VMEM((128, 128), f32)],
+        compiler_params=params(16),
         name="gradient",
     )(gx, thickness, unmix, line, packed, u_vel, v_vel, w_vel)
 

time: 158 us -> 122 us (0.77)
  Pallas kernels: 55.8 us -> 30.8 us
  waiting for transfers between devices: 21.1 us -> 6.68 us
  local copies, waits for them, and re-layouts: 1.31 us -> 5.54 us
  blocking collectives: 63.7 us -> 62 us
    all_to_all x1 -> x0, waiting for transfers between devices: 9.21 us -> none  [on_device(): lax.all_to_all(carries, 'gy', split_axis=0, concat_axis=0, tiled=True)]
    pallas_call x1, Pallas kernels: 15.9 us -> 7.55 us  [on_device(): pl.pallas_call(backward_kernel, out_shape=shape(field, f32), in_specs=[SM...]
    pallas_call x1, Pallas kernels: 16.1 us -> 9.06 us  [on_device(): pl.pallas_call(forward_kernel, out_shape=(shape((32 * ROWS, 128), f32), s...]
    pallas_call x4 -> x2, Pallas kernels: 15.8 us -> 9.03 us  [the longest x1 7.4 us: on_device(): pl.pallas_call(divergence_kernel, out_shape=(shape(field, f32), shape((64...]
    ppermute x0 -> x2, starting transfers between devices: none -> 5.44 us  [the longest x1 5.09 us: on_device(): lax.ppermute(north, 'gy', [(i, (i - 1) % parts) for i in range(parts)])]
    all_to_all x1, waiting for transfers between devices: 11.9 us -> 6.67 us  [on_device(): small = lax.all_to_all(small, 'gy', split_axis=0, concat_axis=0, tiled=True)]
    unnamed x4 -> x46, local copies, waits for them, and re-layouts: 1.31 us -> 5.54 us
    all_to_all x1 -> x0, starting transfers between devices: 3.86 us -> none  [on_device(): lax.all_to_all(carries, 'gy', split_axis=0, concat_axis=0, tiled=True)]
  transfers between devices with their start and end apart: 2 -> 3, of which waited for: 2 -> 1; matrix products, arithmetic and copies ran while one was open for 0% -> 0% of each run, Pallas kernels for 2% -> 1%
where the time goes in v2:
time: 122 us
  blocking collectives  62 us (51%)
  Pallas kernels  30.8 us (25%)
  starting transfers between devices  15.9 us (13%)
  waiting for transfers between devices  6.68 us (5%)
  local copies, waits for them, and re-layouts  5.54 us (5%)
    all_to_all x2, blocking collectives, on_device(): lax.all_to_all(packed, 'gx', split_axis=0, concat_axis=0, tiled=True)  62 us
    all_to_all x1, starting transfers between devices, on_device(): small = lax.all_to_all(small, 'gy', split_axis=0, concat_axis=0, tiled=True)  10.4 us
    pallas_call x1, Pallas kernels, on_device(): pl.pallas_call(forward_kernel, out_shape=(shape((32 * ROWS, 128), f32), s...  9.06 us
    pallas_call x1, Pallas kernels, on_device(): pl.pallas_call(backward_kernel, out_shape=shape(field, f32), in_specs=[SM...  7.55 us
    pallas_call x1, Pallas kernels, on_device(): pl.pallas_call(divergence_kernel, out_shape=(shape(field, f32), shape((64...  7.4 us
    all_to_all x1, waiting for transfers between devices, on_device(): small = lax.all_to_all(small, 'gy', split_axis=0, concat_axis=0, tiled=True)  6.67 us
    unnamed x46, local copies, waits for them, and re-layouts  5.54 us
    pallas_call x1, Pallas kernels, on_device(): pl.pallas_call(gradient_kernel, out_shape=(out, out, out), grid=(4,), in_...  5.2 us
  transfers between devices with their start and end apart: 3, of which 1 were waited for; matrix products, arithmetic and copies ran while one was open for 0% of the time, Pallas kernels for 1%

profile of v2, /device:TPU:2, one launch (start us, length us, event | category | flops | bytes accessed | tf_op | source)
XLA Modules:
  0.0 121.8 jit_solution(9956758220338588237)
XLA Ops:
  0.6 0.0 copy-start
  0.6 1.6 %copy-done = f32[8,512,128]{2,1,0:T(8,128)S(1)} copy-done((f32[8,512,128]{2,1,0:T(8,128)S(1)}, f32[8,512,128]{2,1,0:T(8,128)}, u32[]{:S(2)}) %copy-start) | copy-done | bytes 2097176
  2.2 0.0 copy-start.2
  2.2 1.6 %copy-done.2 = f32[8,512,128]{2,1,0:T(8,128)S(1)} copy-done((f32[8,512,128]{2,1,0:T(8,128)S(1)}, f32[8,512,128]{2,1,0:T(8,128)}, u32[]{:S(2)}) %copy-start.2) | copy-done | bytes 2097176
  3.8 0.0 copy-start.4
  3.8 1.6 %copy-done.4 = f32[8,512,128]{2,1,0:T(8,128)S(1)} copy-done((f32[8,512,128]{2,1,0:T(8,128)S(1)}, f32[8,512,128]{2,1,0:T(8,128)}, u32[]{:S(2)}) %copy-start.4) | copy-done | bytes 2097176
  5.4 0.0 copy-start.20
  5.4 0.7 copy-done.20
  6.1 7.4 %divergence.1 = (f32[8,520,128]{2,1,0:T(8,128)S(1)}, f32[64,128]{1,0:T(8,128)S(1)}, f32[8,128]{1,0:T(8,128)S(1)}) custom-call(s32[1]{0:T(128)} %bitcast.gx_ref, f32[8]{0:T(128)S(1)} %copy-done.20, f32[8,512,128]{2,1,0:T(8,128)S(1)} %copy-done, f32[8,512,128]{2,1,0:T(8,128)S(1)} %copy-done.2, f32[8,512,128]{2,1,0:T(8,128)S(1)} %copy-done.4), custom_call_target="tpu_custom_call" | custom-call | tf_op jit(solution)/shard_map/divergence/pallas_call | solution.py:719
  13.5 0.0 copy-start.8
  13.5 0.0 copy-start.9
  13.5 0.0 copy-start.10
  13.5 0.0 copy-start.11
  13.5 0.0 copy-start.12
  13.5 32.2 %all_to_all.21.in_ref = f32[8,520,128]{2,1,0:T(8,128)S(1)} all-to-all(f32[8,520,128]{2,1,0:T(8,128)S(1)} %get-tuple-element.12), channel_id=1, replica_groups=mesh['gx'=8,'gy'=32] {'gx'}, dimensions={0} | all-to-all | bytes 4259840 | tf_op jit(solution)/shard_map/all_to_all | solution.py:736
  45.8 0.0 copy-start.13
  45.8 0.0 copy-start.14
  45.8 0.0 copy-start.15
  45.8 0.0 copy-start.16
  45.8 0.0 copy-start.17
  45.8 0.0 copy-start.18
  45.8 0.0 copy-start.19
  45.8 0.0 copy-start.21
  45.8 0.0 copy-start.22
  45.9 0.0 copy-start.6
  45.9 0.0 copy-start.7
  45.9 0.0 copy-done.8
  45.9 0.0 copy-done.9
  45.9 0.0 copy-done.10
  45.9 0.0 copy-done.11
  45.9 0.0 copy-done.12
  45.9 9.1 %forward.1 = (f32[4352,128]{1,0:T(8,128)S(1)}, f32[256,128]{1,0:T(8,128)}, f32[32,128]{1,0:T(8,128)S(1)}, f32[32,128]{1,0:T(8,128)S(1)}) custom-call(s32[1]{0:T(128)} %bitcast.gx_ref, f32[8,128]{1,0:T(8,128)S(1)} %get-tuple-element.11.mu_ref, f32[32,128]{1,0:T(8,128)S(1)} %copy-done.12, f32[32,128]{1,0:T(8,128)S(1)} %copy-done.11, f32[32,128]{1,0:T(8,128)S(1)} %copy-done.10, ...), custom_call_target="tpu_custom_call" | custom-call | tf_op jit(solution)/shard_map/forward/pallas_call | solution.py:739
  55.0 10.4 %all-to-all-start.1 = ((f32[32,8,128]{2,1,0:T(8,128)}), f32[32,8,128]{2,1,0:T(8,128)S(1)}, u32[]{:S(2)}, u32[]{:S(2)}) async-start(f32[32,8,128]{2,1,0:T(8,128)} %bitcast.2), calls=%async_computation.1 | async-start | bytes 262144 | tf_op jit(solution)/shard_map/all_to_all | solution.py:753
  65.4 0.4 collective-permute-start
  65.8 5.1 %collective-permute-start.1 = (f32[32,128]{1,0:T(8,128)S(1)}, f32[32,128]{1,0:T(8,128)S(1)}, u32[]{:S(2)}, u32[]{:S(2)}) collective-permute-start(f32[32,128]{1,0:T(8,128)S(1)} %get-tuple-element.15), channel_id=1, source_target_pairs={{0,31},{1,0},{2,1},{3,2},{4,3},{5,4},{6,5},{7,6},{8,7},{9,8},{10,9... | collective-permute-start | bytes 49160 | tf_op jit(solution)/shard_map/ppermute | solution.py:757
  70.8 6.7 %all-to-all-done.1 = f32[32,8,128]{2,1,0:T(8,128)S(1)} async-done(((f32[32,8,128]{2,1,0:T(8,128)}), f32[32,8,128]{2,1,0:T(8,128)S(1)}, u32[]{:S(2)}, u32[]{:S(2)}) %all-to-all-start.1) | async-done | bytes 131104 | tf_op jit(solution)/shard_map/all_to_all | solution.py:753
  77.5 0.0 copy-done.13
  77.5 0.0 copy-done.14
  77.5 0.0 copy-done.15
  77.5 0.0 copy-done.16
  77.5 0.0 copy-done.17
  77.6 0.0 copy-done.18
  77.6 0.0 copy-done.19
  77.6 0.0 copy-done.21
  77.6 0.0 copy-done.22
  77.6 1.6 %line.1.line_ref = f32[104,128]{1,0:T(8,128)S(1)} custom-call(s32[1]{0:T(128)} %bitcast.gx_ref, s32[1]{0:T(128)} %bitcast.1.gy_ref, f32[8]{0:T(128)S(1)} %copy-done.21, f32[8,128]{1,0:T(8,128)S(1)} %get-tuple-element.11.mu_ref, f32[8,128]{1,0:T(8,128)S(1)} %copy-done.22, f32[32,32]{1,0:T(8,128)S(1)} %copy-done.19, f32[32,32]{1,0:T(8,128)S(1)} %copy-done.18, ...), custom_call_target="tpu_custom_call" | custom-call | tf_op jit(solution)/shard_map/line/pallas_call | solution.py:758
  79.2 0.0 collective-permute-done.south_ref
  79.2 0.0 collective-permute-done.1.north_ref
  79.3 0.0 copy-done.6
  79.3 0.0 copy-done.7
  79.3 0.0 copy-start.5
  79.3 7.5 %backward.1 = f32[8,520,128]{2,1,0:T(8,128)S(1)} custom-call(s32[1]{0:T(128)} %bitcast.gx_ref, s32[1]{0:T(128)} %bitcast.1.gy_ref, f32[8,128]{1,0:T(8,128)S(1)} %get-tuple-element.11.mu_ref, f32[32,128]{1,0:T(8,128)S(1)} %copy-done.12, f32[32,128]{1,0:T(8,128)S(1)} %copy-done.11, f32[32,128]{1,0:T(8,128)S(1)} %copy-done.10, bf16[768,256]{1,0:T(8,128)(2,1)S(1)} %copy-done.7, ...), custom_call_target="tpu_custom_call" | custom-call | tf_op jit(solution)/shard_map/backward/pallas_call | solution.py:768
  86.8 0.0 copy-start.1
  86.9 0.0 copy-start.3
  86.9 29.7 %all_to_all.22.p_ref = f32[8,520,128]{2,1,0:T(8,128)S(1)} all-to-all(f32[8,520,128]{2,1,0:T(8,128)S(1)} %backward.1), channel_id=1, replica_groups=mesh['gx'=8,'gy'=32] {'gx'}, dimensions={0} | all-to-all | bytes 4259840 | tf_op jit(solution)/shard_map/all_to_all | solution.py:781
  116.6 0.0 copy-done.5
  116.6 0.0 copy-done.1
  116.6 0.0 copy-done.3
  116.6 5.2 %gradient.1 = (f32[8,512,128]{2,1,0:T(8,128)}, f32[8,512,128]{2,1,0:T(8,128)}, f32[8,512,128]{2,1,0:T(8,128)}) custom-call(s32[1]{0:T(128)} %bitcast.gx_ref, f32[8]{0:T(128)S(1)} %copy-done.21, f32[64,128]{1,0:T(8,128)S(1)} %get-tuple-element.10.unmix_ref, f32[104,128]{1,0:T(8,128)S(1)} %line.1.line_ref, f32[8,520,128]{2,1,0:T(8,128)S(1)} %all_to_all.22.p_ref, ...), custom_call_target="tpu_custom_call" | custom-call | tf_op jit(solution)/shard_map/gradient/pallas_call | solution.py:784
Async XLA Ops:
  0.6 1.6 %copy-start = (f32[8,512,128]{2,1,0:T(8,128)S(1)}, f32[8,512,128]{2,1,0:T(8,128)}, u32[]{:S(2)}) copy-start(f32[8,512,128]{2,1,0:T(8,128)} %u_ref.1) | copy-start | bytes 6291460
  2.2 1.6 %copy-start.2 = (f32[8,512,128]{2,1,0:T(8,128)S(1)}, f32[8,512,128]{2,1,0:T(8,128)}, u32[]{:S(2)}) copy-start(f32[8,512,128]{2,1,0:T(8,128)} %v_ref.1) | copy-start | bytes 6291460
  3.8 1.6 %copy-start.4 = (f32[8,512,128]{2,1,0:T(8,128)S(1)}, f32[8,512,128]{2,1,0:T(8,128)}, u32[]{:S(2)}) copy-start(f32[8,512,128]{2,1,0:T(8,128)} %w_ref.1) | copy-start | bytes 6291460
  5.4 0.7 copy-start.20
  13.5 32.4 %copy-start.8 = (bf16[256,512]{1,0:T(8,128)(2,1)S(1)}, bf16[256,512]{1,0:T(8,128)(2,1)}, u32[]{:S(2)}) copy-start(bf16[256,512]{1,0:T(8,128)(2,1)} %constant.43.clone.first_ref) | copy-start | bytes 786436
  13.5 32.4 %copy-start.9 = (bf16[256,512]{1,0:T(8,128)(2,1)S(1)}, bf16[256,512]{1,0:T(8,128)(2,1)}, u32[]{:S(2)}) copy-start(bf16[256,512]{1,0:T(8,128)(2,1)} %constant.42.clone.common_ref) | copy-start | bytes 786436
  13.5 32.4 %copy-start.10 = (f32[32,128]{1,0:T(8,128)S(1)}, f32[32,128]{1,0:T(8,128)}, u32[]{:S(2)}) copy-start(f32[32,128]{1,0:T(8,128)} %constant.41.clone.ts_ref) | copy-start | bytes 49156
  13.5 32.4 %copy-start.11 = (f32[32,128]{1,0:T(8,128)S(1)}, f32[32,128]{1,0:T(8,128)}, u32[]{:S(2)}) copy-start(f32[32,128]{1,0:T(8,128)} %constant.40.clone.tc_ref) | copy-start | bytes 49156
  13.5 32.4 %copy-start.12 = (f32[32,128]{1,0:T(8,128)S(1)}, f32[32,128]{1,0:T(8,128)}, u32[]{:S(2)}) copy-start(f32[32,128]{1,0:T(8,128)} %constant.39.clone.sines_ref) | copy-start | bytes 49156
  45.8 31.7 %copy-start.13 = (f32[128,128]{1,0:T(8,128)S(1)}, f32[128,128]{1,0:T(8,128)}, u32[]{:S(2)}) copy-start(f32[128,128]{1,0:T(8,128)} %constant.50.clone.s128_ref) | copy-start | bytes 196612
  45.8 31.7 %copy-start.14 = (f32[128,128]{1,0:T(8,128)S(1)}, f32[128,128]{1,0:T(8,128)}, u32[]{:S(2)}) copy-start(f32[128,128]{1,0:T(8,128)} %constant.49.clone.c128_ref) | copy-start | bytes 196612
  45.8 31.7 %copy-start.15 = (f32[32,128]{1,0:T(8,128)S(1)}, f32[32,128]{1,0:T(8,128)}, u32[]{:S(2)}) copy-start(f32[32,128]{1,0:T(8,128)} %constant.51.clone.lam_ref) | copy-start | bytes 49156
  45.8 31.8 %copy-start.16 = (f32[32,128]{1,0:T(8,128)S(1)}, f32[32,128]{1,0:T(8,128)}, u32[]{:S(2)}) copy-start(f32[32,128]{1,0:T(8,128)} %constant.48.clone.ts_ref) | copy-start | bytes 49156
  45.8 31.8 %copy-start.17 = (f32[32,128]{1,0:T(8,128)S(1)}, f32[32,128]{1,0:T(8,128)}, u32[]{:S(2)}) copy-start(f32[32,128]{1,0:T(8,128)} %constant.47.clone.tc_ref) | copy-start | bytes 49156
  45.8 31.8 %copy-start.18 = (f32[32,32]{1,0:T(8,128)S(1)}, f32[32,32]{1,0:T(8,128)}, u32[]{:S(2)}) copy-start(f32[32,32]{1,0:T(8,128)} %constant.46.clone.s32_ref) | copy-start | bytes 12292
  45.8 31.8 %copy-start.19 = (f32[32,32]{1,0:T(8,128)S(1)}, f32[32,32]{1,0:T(8,128)}, u32[]{:S(2)}) copy-start(f32[32,32]{1,0:T(8,128)} %constant.45.clone.c32_ref) | copy-start | bytes 12292
  45.8 31.7 %copy-start.21 = (f32[8]{0:T(128)S(1)}, f32[8]{0:T(128)}, u32[]{:S(2)}) copy-start(f32[8]{0:T(128)} %thick_ref.5) | copy-start | bytes 100
  45.8 31.7 %copy-start.22 = (f32[8,128]{1,0:T(8,128)S(1)}, f32[8,128]{1,0:T(8,128)}, u32[]{:S(2)}) copy-start(f32[8,128]{1,0:T(8,128)} %constant.44.clone.slow_ref) | copy-start | bytes 12292
  45.9 33.4 %copy-start.6 = (bf16[768,256]{1,0:T(8,128)(2,1)S(1)}, bf16[768,256]{1,0:T(8,128)(2,1)}, u32[]{:S(2)}) copy-start(bf16[768,256]{1,0:T(8,128)(2,1)} %constant.53.clone.first_ref) | copy-start | bytes 1179652
  45.9 33.4 %copy-start.7 = (bf16[768,256]{1,0:T(8,128)(2,1)S(1)}, bf16[768,256]{1,0:T(8,128)(2,1)}, u32[]{:S(2)}) copy-start(bf16[768,256]{1,0:T(8,128)(2,1)} %constant.52.clone.common_ref) | copy-start | bytes 1179652
  55.0 22.5 %all-to-all-start.1 = ((f32[32,8,128]{2,1,0:T(8,128)}), f32[32,8,128]{2,1,0:T(8,128)S(1)}, u32[]{:S(2)}, u32[]{:S(2)}) async-start(f32[32,8,128]{2,1,0:T(8,128)} %bitcast.2), calls=%async_computation.1 | async-start | bytes 262144 | tf_op jit(solution)/shard_map/all_to_all | solution.py:753
  65.4 13.8 %collective-permute-start = (f32[32,128]{1,0:T(8,128)S(1)}, f32[32,128]{1,0:T(8,128)S(1)}, u32[]{:S(2)}, u32[]{:S(2)}) collective-permute-start(f32[32,128]{1,0:T(8,128)S(1)} %get-tuple-element.14), channel_id=1, source_target_pairs={{0,1},{1,2},{2,3},{3,4},{4,5},{5,6},{6,7},{7,8},{8,9},{9,10},{10,1... | collective-permute-start | bytes 49160 | tf_op jit(solution)/shard_map/ppermute | solution.py:756
  65.8 13.5 %collective-permute-start.1 = (f32[32,128]{1,0:T(8,128)S(1)}, f32[32,128]{1,0:T(8,128)S(1)}, u32[]{:S(2)}, u32[]{:S(2)}) collective-permute-start(f32[32,128]{1,0:T(8,128)S(1)} %get-tuple-element.15), channel_id=1, source_target_pairs={{0,31},{1,0},{2,1},{3,2},{4,3},{5,4},{6,5},{7,6},{8,7},{9,8},{10,9... | collective-permute-start | bytes 49160 | tf_op jit(solution)/shard_map/ppermute | solution.py:757
  79.3 37.3 %copy-start.5 = (f32[8,512,128]{2,1,0:T(8,128)S(1)}, f32[8,512,128]{2,1,0:T(8,128)}, u32[]{:S(2)}) copy-start(f32[8,512,128]{2,1,0:T(8,128)} %w_ref.1) | copy-start | bytes 6291460
  86.8 29.7 %copy-start.1 = (f32[8,512,128]{2,1,0:T(8,128)S(1)}, f32[8,512,128]{2,1,0:T(8,128)}, u32[]{:S(2)}) copy-start(f32[8,512,128]{2,1,0:T(8,128)} %u_ref.1) | copy-start | bytes 6291460
  86.9 29.7 %copy-start.3 = (f32[8,512,128]{2,1,0:T(8,128)S(1)}, f32[8,512,128]{2,1,0:T(8,128)}, u32[]{:S(2)}) copy-start(f32[8,512,128]{2,1,0:T(8,128)} %v_ref.1) | copy-start | bytes 6291460

commit v3 on v2

--- a/solution.py
+++ b/solution.py
@@ -239,7 +239,7 @@
 for _ in range(7):
     ROUNDS.append([tuple(sorted((_seats[i], _seats[7 - i]))) for i in range(4)])
     _seats = [_seats[0], _seats[7]] + _seats[1:7]
-SWEEPS = 6
+SWEEPS = 5
 PAIRS = [(i, j) for i in range(8) for j in range(i, 8)]
 
 
@@ -274,35 +274,36 @@
             for p, q in pairs:
                 off = a[(p, q)]
                 diff = a[(q, q)] - a[(p, p)]
-                size = jnp.sqrt(diff * diff + 4.0 * off * off)
-                low = jnp.where(diff < 0.0, diff - size, diff + size)
-                tan = 2.0 * off / jnp.where(low == 0.0, 1.0, low)
-                cos = 1.0 / jnp.sqrt(1.0 + tan * tan)
-                turn[(p, q)] = (cos, tan * cos, tan)
-            full = [[get(i, j) for j in range(8)] for i in range(8)]
-            for p, q in pairs:
-                cos, sin, _t = turn[(p, q)]
+                twice = 2.0 * off
+                square = diff * diff + twice * twice
+                some = square > 0.0
+                inv = lax.rsqrt(jnp.where(some, square, 1.0))
+                both = 0.5 + 0.5 * jnp.where(some, jnp.abs(diff) * inv, 1.0)
+                over = lax.rsqrt(both)
+                cos = both * over
+                sin = 0.5 * jnp.where(diff < 0.0, -twice, twice) * (inv * over)
+                tan = sin * over
+                turn[(p, q)] = (cos, sin, tan)
+            new = {}
+            for n, (p, q) in enumerate(pairs):
+                cos, sin, tan = turn[(p, q)]
+                off = a[(p, q)]
+                new[(p, p)] = a[(p, p)] - tan * off
+                new[(q, q)] = a[(q, q)] + tan * off
+                new[(p, q)] = zero
                 for i in range(8):
-                    x, y = full[i][p], full[i][q]
-                    full[i][p], full[i][q] = cos * x - sin * y, sin * x + cos * y
                     x, y = vec[i][p], vec[i][q]
                     vec[i][p], vec[i][q] = cos * x - sin * y, sin * x + cos * y
-            for p, q in pairs:
-                cos, sin, tan = turn[(p, q)]
-                for j in range(8):
-                    x, y = full[p][j], full[q][j]
-                    full[p][j], full[q][j] = cos * x - sin * y, sin * x + cos * y
-            diag = {}
-            for p, q in pairs:
-                cos, sin, tan = turn[(p, q)]
-                off = a[(p, q)]
-                diag[p] = a[(p, p)] - tan * off
-                diag[q] = a[(q, q)] + tan * off
-            a = {(i, j): full[i][j] for i, j in PAIRS}
-            for p, q in pairs:
-                a[(p, q)] = zero
-            for p in diag:
-                a[(p, p)] = diag[p]
+                for r, s in pairs[n + 1 :]:
+                    cos2, sin2, _t = turn[(r, s)]
+                    half = []
+                    for i in (p, q):
+                        x, y = get(i, r), get(i, s)
+                        half.append((cos2 * x - sin2 * y, sin2 * x + cos2 * y))
+                    for j, x, y in ((r, half[0][0], half[1][0]), (s, half[0][1], half[1][1])):
+                        new[tuple(sorted((p, j)))] = cos * x - sin * y
+                        new[tuple(sorted((q, j)))] = sin * x + cos * y
+            a = new
         return tuple(a[pair] for pair in PAIRS), tuple(vec[i][j] for i in range(8) for j in range(8))
 
     start = (tuple(a[pair] for pair in PAIRS), tuple(vec[i][j] for i in range(8) for j in range(8)))
@@ -415,7 +416,7 @@
 
 def forward_kernel(
     gx_ref, mu_ref, sines_ref, tc_ref, ts_ref, common_ref, first_ref, in_ref, out_ref, small_ref,
-    south_ref, north_ref, grid_ref, y_ref, side_ref, turn_ref,
+    south_ref, north_ref, grid_ref, y_ref, raw_ref, side_ref, turn_ref,
 ):
     row8 = iota((8, 128), 0)
     row128 = iota((128, 128), 0)
@@ -447,35 +448,37 @@
 
     def product(n, carry):
         start = pl.multiple_of(n * batch, 8)
-        out_ref[pl.ds(start, batch), :] = forward_product(y_ref[pl.ds(start, batch), :], common_ref)
+        raw_ref[pl.ds(start, batch), :] = forward_product(y_ref[pl.ds(start, batch), :], common_ref)
         return carry
 
     lax.fori_loop(0, 32 // BATCH, product, 0)
-    out_ref[0:144, :] = jnp.where(
-        iota((144, 128), 0) < ROWS, forward_product(y_ref[0:144, :], first_ref), out_ref[0:144, :]
+    raw_ref[0:144, :] = jnp.where(
+        iota((144, 128), 0) < ROWS, forward_product(y_ref[0:144, :], first_ref), raw_ref[0:144, :]
     )
 
-    line = out_ref[0:128, :].T[0:1]
-    ghost_line = out_ref[128:129, :]
+    line = raw_ref[0:128, :].T[0:1]
+    ghost_line = raw_ref[128:129, :]
 
     eigen = eigen_table(sines_ref[...], mu_ref[pl.ds(gx_ref[0], 1), :], True)
     rho, gap, _ = decay(eigen)
-    ghost = out_ref[pl.ds(128, 32, stride=ROWS), :]
+    ghost = raw_ref[pl.ds(128, 32, stride=ROWS), :]
 
     def from_north(n, b):
         j = 127 - n
         side_ref[pl.ds(j, 32, stride=ROWS), :] = rho * b
-        return out_ref[pl.ds(j, 32, stride=ROWS), :] + (b - gap * b)
+        return raw_ref[pl.ds(j, 32, stride=ROWS), :] + (b - gap * b)
 
     b = lax.fori_loop(0, 128, from_north, ghost, unroll=8)
 
     def from_south(j, f):
-        f = out_ref[pl.ds(j, 32, stride=ROWS), :] + (f - gap * f)
+        f = raw_ref[pl.ds(j, 32, stride=ROWS), :] + (f - gap * f)
         out_ref[pl.ds(j, 32, stride=ROWS), :] = f + side_ref[pl.ds(j, 32, stride=ROWS), :]
         return f
 
     f = lax.fori_loop(0, 128, from_south, jnp.zeros((32, 128), f32), unroll=8)
     out_ref[pl.ds(128, 32, stride=ROWS), :] = rho * f + ghost
+    for r in range(129, ROWS):
+        out_ref[pl.ds(r, 32, stride=ROWS), :] = jnp.zeros((32, 128), f32)
 
     totals = in_ref[0, 517:518, :]
     for s in range(1, 8):
@@ -574,7 +577,7 @@
 
 def backward_kernel(
     gx_ref, gy_ref, mu_ref, sines_ref, tc_ref, ts_ref, common_ref, first_ref, line_ref, south_ref,
-    north_ref, in_ref, out_ref, p_ref, z_ref, grid_ref,
+    north_ref, in_ref, out_ref, half_ref, p_ref, z_ref, grid_ref,
 ):
     eigen = eigen_table(sines_ref[...], mu_ref[pl.ds(gx_ref[0], 1), :], True)
     rho, gap, factor = decay(eigen)
@@ -586,7 +589,7 @@
 
     def from_south(j, c):
         c = c - gap * c
-        p_ref[pl.ds(j, 32, stride=ROWS), :] = in_ref[pl.ds(j, 32, stride=ROWS), :] + c
+        half_ref[pl.ds(j, 32, stride=ROWS), :] = in_ref[pl.ds(j, 32, stride=ROWS), :] + c
         return c
 
     c = lax.fori_loop(0, 128, from_south, south, unroll=8)
@@ -596,7 +599,7 @@
     def from_north(n, h):
         j = 127 - n
         h = h - gap * h
-        p_ref[pl.ds(j, 32, stride=ROWS), :] = (p_ref[pl.ds(j, 32, stride=ROWS), :] + h) * factor
+        p_ref[pl.ds(j, 32, stride=ROWS), :] = (half_ref[pl.ds(j, 32, stride=ROWS), :] + h) * factor
         return h
 
     lax.fori_loop(0, 128, from_north, north, unroll=8)
@@ -732,7 +735,7 @@
         ],
         compiler_params=params(12),
         name="divergence",
-    )(gx, thickness, u_vel, v_vel, w_vel)
+    )(gx, thickness, *[pltpu.with_memory_space_constraint(x, pltpu.HBM) for x in (u_vel, v_vel, w_vel)])
     packed = lax.all_to_all(packed, "gx", split_axis=0, concat_axis=0, tiled=True)
 
     rows = shape((32, 128), f32)
@@ -744,6 +747,7 @@
         scratch_shapes=[
             pltpu.VMEM((32, ROWS, 128), f32),
             pltpu.VMEM((32 * ROWS, 256), f32),
+            pltpu.VMEM((32 * ROWS, 128), f32),
             pltpu.VMEM((32 * ROWS, 128), f32),
             pltpu.VMEM((128, 128), f32),
         ],
@@ -773,6 +777,7 @@
         compiler_params=params(20),
         scratch_shapes=[
             pltpu.VMEM((32 * ROWS, 128), f32),
+            pltpu.VMEM((32 * ROWS, 128), f32),
             pltpu.VMEM((32 * ROWS, 256), f32),
             pltpu.VMEM((32, ROWS, 128), f32),
         ],

time: 122 us -> 115 us (0.943)
  local copies, waits for them, and re-layouts: 5.54 us -> 0.77 us
  Pallas kernels: 30.8 us -> 29 us
    unnamed x46 -> x40, local copies, waits for them, and re-layouts: 5.54 us -> 0.77 us
    pallas_call x1, Pallas kernels: 7.4 us -> 5.87 us  [on_device(): pl.pallas_call(divergence_kernel, out_shape=(shape(field, f32), shape((64...]
where the time goes in v3:
time: 115 us
  blocking collectives  62 us (54%)
  Pallas kernels  29 us (25%)
  starting transfers between devices  15.9 us (14%)
  waiting for transfers between devices  6.68 us (6%)
    all_to_all x2, blocking collectives, on_device(): lax.all_to_all(packed, 'gx', split_axis=0, concat_axis=0, tiled=True)  62 us
    all_to_all x1, starting transfers between devices, on_device(): small = lax.all_to_all(small, 'gy', split_axis=0, concat_axis=0, tiled=True)  10.4 us
    pallas_call x1, Pallas kernels, on_device(): pl.pallas_call(forward_kernel, out_shape=(shape((32 * ROWS, 128), f32), s...  9.02 us
    pallas_call x1, Pallas kernels, on_device(): pl.pallas_call(backward_kernel, out_shape=shape(field, f32), in_specs=[SM...  7.28 us
    all_to_all x1, waiting for transfers between devices, on_device(): small = lax.all_to_all(small, 'gy', split_axis=0, concat_axis=0, tiled=True)  6.67 us
    pallas_call x1, Pallas kernels, on_device(): pl.pallas_call(divergence_kernel, out_shape=(shape(field, f32), shape((64...  5.87 us
    pallas_call x1, Pallas kernels, on_device(): pl.pallas_call(gradient_kernel, out_shape=(out, out, out), grid=(4,), in_...  5.2 us
    ppermute x1, starting transfers between devices, on_device(): lax.ppermute(north, 'gy', [(i, (i - 1) % parts) for i in range(parts)])  5.09 us
  transfers between devices with their start and end apart: 3, of which 1 were waited for; matrix products, arithmetic and copies ran while one was open for 0% of the time, Pallas kernels for 1%

profile of v3, /device:TPU:2, one launch (start us, length us, event | category | flops | bytes accessed | tf_op | source)
XLA Modules:
  0.0 115.2 jit_solution(10235437715631301434)
XLA Ops:
  0.6 0.0 copy-start.17
  0.6 0.6 copy-done.17
  1.3 5.9 %divergence.1 = (f32[8,520,128]{2,1,0:T(8,128)S(1)}, f32[64,128]{1,0:T(8,128)S(1)}, f32[8,128]{1,0:T(8,128)S(1)}) custom-call(s32[1]{0:T(128)} %bitcast.gx_ref, f32[8]{0:T(128)S(1)} %copy-done.17, f32[8,512,128]{2,1,0:T(8,128)} %u_ref.1, f32[8,512,128]{2,1,0:T(8,128)} %v_ref.1, f32[8,512,128]{2,1,0:T(8,128)} %w_ref.1), custom_call_target="tpu_custom_call" | custom-call | tf_op jit(solution)/shard_map/divergence/pallas_call | solution.py:722
  7.2 0.0 copy-start.5
  7.2 0.0 copy-start.6
  7.2 0.0 copy-start.7
  7.2 0.0 copy-start.8
  7.2 0.0 copy-start.9
  7.2 32.2 %all_to_all.21.in_ref = f32[8,520,128]{2,1,0:T(8,128)S(1)} all-to-all(f32[8,520,128]{2,1,0:T(8,128)S(1)} %get-tuple-element.12), channel_id=1, replica_groups=mesh['gx'=8,'gy'=32] {'gx'}, dimensions={0} | all-to-all | bytes 4259840 | tf_op jit(solution)/shard_map/all_to_all | solution.py:739
  39.5 0.0 copy-start.10
  39.5 0.0 copy-start.11
  39.5 0.0 copy-start.12
  39.5 0.0 copy-start.13
  39.5 0.0 copy-start.14
  39.5 0.0 copy-start.15
  39.5 0.0 copy-start.16
  39.5 0.0 copy-start.18
  39.5 0.0 copy-start.19
  39.5 0.0 copy-start.3
  39.6 0.0 copy-start.4
  39.6 0.0 copy-done.5
  39.6 0.0 copy-done.6
  39.6 0.0 copy-done.7
  39.6 0.0 copy-done.8
  39.6 0.0 copy-done.9
  39.6 9.0 %forward.1 = (f32[4352,128]{1,0:T(8,128)S(1)}, f32[256,128]{1,0:T(8,128)}, f32[32,128]{1,0:T(8,128)S(1)}, f32[32,128]{1,0:T(8,128)S(1)}) custom-call(s32[1]{0:T(128)} %bitcast.gx_ref, f32[8,128]{1,0:T(8,128)S(1)} %get-tuple-element.11.mu_ref, f32[32,128]{1,0:T(8,128)S(1)} %copy-done.9, f32[32,128]{1,0:T(8,128)S(1)} %copy-done.8, f32[32,128]{1,0:T(8,128)S(1)} %copy-done.7, ...), custom_call_target="tpu_custom_call" | custom-call | tf_op jit(solution)/shard_map/forward/pallas_call | solution.py:742
  48.6 10.4 %all-to-all-start.1 = ((f32[32,8,128]{2,1,0:T(8,128)}), f32[32,8,128]{2,1,0:T(8,128)S(1)}, u32[]{:S(2)}, u32[]{:S(2)}) async-start(f32[32,8,128]{2,1,0:T(8,128)} %bitcast.2), calls=%async_computation.1 | async-start | bytes 262144 | tf_op jit(solution)/shard_map/all_to_all | solution.py:757
  59.1 0.4 collective-permute-start
  59.4 5.1 %collective-permute-start.1 = (f32[32,128]{1,0:T(8,128)S(1)}, f32[32,128]{1,0:T(8,128)S(1)}, u32[]{:S(2)}, u32[]{:S(2)}) collective-permute-start(f32[32,128]{1,0:T(8,128)S(1)} %get-tuple-element.15), channel_id=1, source_target_pairs={{0,31},{1,0},{2,1},{3,2},{4,3},{5,4},{6,5},{7,6},{8,7},{9,8},{10,9... | collective-permute-start | bytes 49160 | tf_op jit(solution)/shard_map/ppermute | solution.py:761
  64.5 6.7 %all-to-all-done.1 = f32[32,8,128]{2,1,0:T(8,128)S(1)} async-done(((f32[32,8,128]{2,1,0:T(8,128)}), f32[32,8,128]{2,1,0:T(8,128)S(1)}, u32[]{:S(2)}, u32[]{:S(2)}) %all-to-all-start.1) | async-done | bytes 131104 | tf_op jit(solution)/shard_map/all_to_all | solution.py:757
  71.2 0.0 copy-done.10
  71.2 0.0 copy-done.11
  71.2 0.0 copy-done.12
  71.2 0.0 copy-done.13
  71.2 0.0 copy-done.14
  71.2 0.0 copy-done.15
  71.2 0.0 copy-done.16
  71.2 0.0 copy-done.18
  71.2 0.0 copy-done.19
  71.2 1.6 %line.1.line_ref = f32[104,128]{1,0:T(8,128)S(1)} custom-call(s32[1]{0:T(128)} %bitcast.gx_ref, s32[1]{0:T(128)} %bitcast.1.gy_ref, f32[8]{0:T(128)S(1)} %copy-done.18, f32[8,128]{1,0:T(8,128)S(1)} %get-tuple-element.11.mu_ref, f32[8,128]{1,0:T(8,128)S(1)} %copy-done.19, f32[32,32]{1,0:T(8,128)S(1)} %copy-done.16, f32[32,32]{1,0:T(8,128)S(1)} %copy-done.15, ...), custom_call_target="tpu_custom_call" | custom-call | tf_op jit(solution)/shard_map/line/pallas_call | solution.py:762
  72.9 0.0 collective-permute-done.south_ref
  72.9 0.0 collective-permute-done.1.north_ref
  72.9 0.0 copy-done.3
  72.9 0.0 copy-done.4
  72.9 0.0 copy-start.2
  72.9 7.3 %backward.1 = f32[8,520,128]{2,1,0:T(8,128)S(1)} custom-call(s32[1]{0:T(128)} %bitcast.gx_ref, s32[1]{0:T(128)} %bitcast.1.gy_ref, f32[8,128]{1,0:T(8,128)S(1)} %get-tuple-element.11.mu_ref, f32[32,128]{1,0:T(8,128)S(1)} %copy-done.9, f32[32,128]{1,0:T(8,128)S(1)} %copy-done.8, f32[32,128]{1,0:T(8,128)S(1)} %copy-done.7, bf16[768,256]{1,0:T(8,128)(2,1)S(1)} %copy-done.4, ...), custom_call_target="tpu_custom_call" | custom-call | tf_op jit(solution)/shard_map/backward/pallas_call | solution.py:772
  80.2 0.0 copy-start
  80.2 0.0 copy-start.1
  80.3 29.7 %all_to_all.22.p_ref = f32[8,520,128]{2,1,0:T(8,128)S(1)} all-to-all(f32[8,520,128]{2,1,0:T(8,128)S(1)} %backward.1), channel_id=1, replica_groups=mesh['gx'=8,'gy'=32] {'gx'}, dimensions={0} | all-to-all | bytes 4259840 | tf_op jit(solution)/shard_map/all_to_all | solution.py:786
  110.0 0.0 copy-done.2
  110.0 0.0 copy-done
  110.0 0.0 copy-done.1
  110.0 5.2 %gradient.1 = (f32[8,512,128]{2,1,0:T(8,128)}, f32[8,512,128]{2,1,0:T(8,128)}, f32[8,512,128]{2,1,0:T(8,128)}) custom-call(s32[1]{0:T(128)} %bitcast.gx_ref, f32[8]{0:T(128)S(1)} %copy-done.18, f32[64,128]{1,0:T(8,128)S(1)} %get-tuple-element.10.unmix_ref, f32[104,128]{1,0:T(8,128)S(1)} %line.1.line_ref, f32[8,520,128]{2,1,0:T(8,128)S(1)} %all_to_all.22.p_ref, ...), custom_call_target="tpu_custom_call" | custom-call | tf_op jit(solution)/shard_map/gradient/pallas_call | solution.py:789
Async XLA Ops:
  0.6 0.7 copy-start.17
  7.2 32.4 %copy-start.5 = (bf16[256,512]{1,0:T(8,128)(2,1)S(1)}, bf16[256,512]{1,0:T(8,128)(2,1)}, u32[]{:S(2)}) copy-start(bf16[256,512]{1,0:T(8,128)(2,1)} %constant.43.clone.first_ref) | copy-start | bytes 786436
  7.2 32.4 %copy-start.6 = (bf16[256,512]{1,0:T(8,128)(2,1)S(1)}, bf16[256,512]{1,0:T(8,128)(2,1)}, u32[]{:S(2)}) copy-start(bf16[256,512]{1,0:T(8,128)(2,1)} %constant.42.clone.common_ref) | copy-start | bytes 786436
  7.2 32.4 %copy-start.7 = (f32[32,128]{1,0:T(8,128)S(1)}, f32[32,128]{1,0:T(8,128)}, u32[]{:S(2)}) copy-start(f32[32,128]{1,0:T(8,128)} %constant.41.clone.ts_ref) | copy-start | bytes 49156
  7.2 32.4 %copy-start.8 = (f32[32,128]{1,0:T(8,128)S(1)}, f32[32,128]{1,0:T(8,128)}, u32[]{:S(2)}) copy-start(f32[32,128]{1,0:T(8,128)} %constant.40.clone.tc_ref) | copy-start | bytes 49156
  7.2 32.4 %copy-start.9 = (f32[32,128]{1,0:T(8,128)S(1)}, f32[32,128]{1,0:T(8,128)}, u32[]{:S(2)}) copy-start(f32[32,128]{1,0:T(8,128)} %constant.39.clone.sines_ref) | copy-start | bytes 49156
  39.5 31.7 %copy-start.10 = (f32[128,128]{1,0:T(8,128)S(1)}, f32[128,128]{1,0:T(8,128)}, u32[]{:S(2)}) copy-start(f32[128,128]{1,0:T(8,128)} %constant.50.clone.s128_ref) | copy-start | bytes 196612
  39.5 31.7 %copy-start.11 = (f32[128,128]{1,0:T(8,128)S(1)}, f32[128,128]{1,0:T(8,128)}, u32[]{:S(2)}) copy-start(f32[128,128]{1,0:T(8,128)} %constant.49.clone.c128_ref) | copy-start | bytes 196612
  39.5 31.7 %copy-start.12 = (f32[32,128]{1,0:T(8,128)S(1)}, f32[32,128]{1,0:T(8,128)}, u32[]{:S(2)}) copy-start(f32[32,128]{1,0:T(8,128)} %constant.51.clone.lam_ref) | copy-start | bytes 49156
  39.5 31.7 %copy-start.13 = (f32[32,128]{1,0:T(8,128)S(1)}, f32[32,128]{1,0:T(8,128)}, u32[]{:S(2)}) copy-start(f32[32,128]{1,0:T(8,128)} %constant.48.clone.ts_ref) | copy-start | bytes 49156
  39.5 31.7 %copy-start.14 = (f32[32,128]{1,0:T(8,128)S(1)}, f32[32,128]{1,0:T(8,128)}, u32[]{:S(2)}) copy-start(f32[32,128]{1,0:T(8,128)} %constant.47.clone.tc_ref) | copy-start | bytes 49156
  39.5 31.7 %copy-start.15 = (f32[32,32]{1,0:T(8,128)S(1)}, f32[32,32]{1,0:T(8,128)}, u32[]{:S(2)}) copy-start(f32[32,32]{1,0:T(8,128)} %constant.46.clone.s32_ref) | copy-start | bytes 12292
  39.5 31.7 %copy-start.16 = (f32[32,32]{1,0:T(8,128)S(1)}, f32[32,32]{1,0:T(8,128)}, u32[]{:S(2)}) copy-start(f32[32,32]{1,0:T(8,128)} %constant.45.clone.c32_ref) | copy-start | bytes 12292
  39.5 31.7 %copy-start.18 = (f32[8]{0:T(128)S(1)}, f32[8]{0:T(128)}, u32[]{:S(2)}) copy-start(f32[8]{0:T(128)} %thick_ref.5) | copy-start | bytes 100
  39.5 31.7 %copy-start.19 = (f32[8,128]{1,0:T(8,128)S(1)}, f32[8,128]{1,0:T(8,128)}, u32[]{:S(2)}) copy-start(f32[8,128]{1,0:T(8,128)} %constant.44.clone.slow_ref) | copy-start | bytes 12292
  39.5 33.4 %copy-start.3 = (bf16[768,256]{1,0:T(8,128)(2,1)S(1)}, bf16[768,256]{1,0:T(8,128)(2,1)}, u32[]{:S(2)}) copy-start(bf16[768,256]{1,0:T(8,128)(2,1)} %constant.53.clone.first_ref) | copy-start | bytes 1179652
  39.6 33.4 %copy-start.4 = (bf16[768,256]{1,0:T(8,128)(2,1)S(1)}, bf16[768,256]{1,0:T(8,128)(2,1)}, u32[]{:S(2)}) copy-start(bf16[768,256]{1,0:T(8,128)(2,1)} %constant.52.clone.common_ref) | copy-start | bytes 1179652
  48.6 22.5 %all-to-all-start.1 = ((f32[32,8,128]{2,1,0:T(8,128)}), f32[32,8,128]{2,1,0:T(8,128)S(1)}, u32[]{:S(2)}, u32[]{:S(2)}) async-start(f32[32,8,128]{2,1,0:T(8,128)} %bitcast.2), calls=%async_computation.1 | async-start | bytes 262144 | tf_op jit(solution)/shard_map/all_to_all | solution.py:757
  59.1 13.8 %collective-permute-start = (f32[32,128]{1,0:T(8,128)S(1)}, f32[32,128]{1,0:T(8,128)S(1)}, u32[]{:S(2)}, u32[]{:S(2)}) collective-permute-start(f32[32,128]{1,0:T(8,128)S(1)} %get-tuple-element.14), channel_id=1, source_target_pairs={{0,1},{1,2},{2,3},{3,4},{4,5},{5,6},{6,7},{7,8},{8,9},{9,10},{10,1... | collective-permute-start | bytes 49160 | tf_op jit(solution)/shard_map/ppermute | solution.py:760
  59.4 13.5 %collective-permute-start.1 = (f32[32,128]{1,0:T(8,128)S(1)}, f32[32,128]{1,0:T(8,128)S(1)}, u32[]{:S(2)}, u32[]{:S(2)}) collective-permute-start(f32[32,128]{1,0:T(8,128)S(1)} %get-tuple-element.15), channel_id=1, source_target_pairs={{0,31},{1,0},{2,1},{3,2},{4,3},{5,4},{6,5},{7,6},{8,7},{9,8},{10,9... | collective-permute-start | bytes 49160 | tf_op jit(solution)/shard_map/ppermute | solution.py:761
  72.9 37.1 %copy-start.2 = (f32[8,512,128]{2,1,0:T(8,128)S(1)}, f32[8,512,128]{2,1,0:T(8,128)}, u32[]{:S(2)}) copy-start(f32[8,512,128]{2,1,0:T(8,128)} %w_ref.1) | copy-start | bytes 6291460
  80.2 29.8 %copy-start = (f32[8,512,128]{2,1,0:T(8,128)S(1)}, f32[8,512,128]{2,1,0:T(8,128)}, u32[]{:S(2)}) copy-start(f32[8,512,128]{2,1,0:T(8,128)} %u_ref.1) | copy-start | bytes 6291460
  80.2 29.7 %copy-start.1 = (f32[8,512,128]{2,1,0:T(8,128)S(1)}, f32[8,512,128]{2,1,0:T(8,128)}, u32[]{:S(2)}) copy-start(f32[8,512,128]{2,1,0:T(8,128)} %v_ref.1) | copy-start | bytes 6291460

commit v4 on v3

--- a/solution.py
+++ b/solution.py
@@ -259,12 +259,16 @@
         if k > 0:
             total = total + unit / (t[k] * centre[k - 1])
         a[(k, k)] = -total
-    vec = [[one if i == j else zero for j in range(8)] for i in range(8)]
+    place = iota((8, 128), 0)
+    vec = [jnp.where(place == j, one, zero) for j in range(8)]
+    scale = root[0]
+    for k in range(1, 8):
+        scale = jnp.where(place == k, root[k], scale)
 
     def sweep(_, carry):
         flat_a, flat_v = carry
         a = dict(zip(PAIRS, flat_a))
-        vec = [list(flat_v[8 * i : 8 * i + 8]) for i in range(8)]
+        vec = list(flat_v)
 
         def get(i, j):
             return a[(i, j) if i <= j else (j, i)]
@@ -291,9 +295,8 @@
                 new[(p, p)] = a[(p, p)] - tan * off
                 new[(q, q)] = a[(q, q)] + tan * off
                 new[(p, q)] = zero
-                for i in range(8):
-                    x, y = vec[i][p], vec[i][q]
-                    vec[i][p], vec[i][q] = cos * x - sin * y, sin * x + cos * y
+                x, y = vec[p], vec[q]
+                vec[p], vec[q] = cos * x - sin * y, sin * x + cos * y
                 for r, s in pairs[n + 1 :]:
                     cos2, sin2, _t = turn[(r, s)]
                     half = []
@@ -304,17 +307,15 @@
                         new[tuple(sorted((p, j)))] = cos * x - sin * y
                         new[tuple(sorted((q, j)))] = sin * x + cos * y
             a = new
-        return tuple(a[pair] for pair in PAIRS), tuple(vec[i][j] for i in range(8) for j in range(8))
-
-    start = (tuple(a[pair] for pair in PAIRS), tuple(vec[i][j] for i in range(8) for j in range(8)))
+        return tuple(a[pair] for pair in PAIRS), tuple(vec)
+
+    start = (tuple(a[pair] for pair in PAIRS), tuple(vec))
     flat_a, flat_v = lax.fori_loop(0, SWEEPS, sweep, start)
     a = dict(zip(PAIRS, flat_a))
     for mode in range(8):
         mu_ref[mode : mode + 1, :] = jnp.minimum(a[(mode, mode)] * (1.0 / unit), 0.0)[0:1]
-        for k in range(8):
-            entry = flat_v[8 * k + mode]
-            mix_ref[8 * mode + k : 8 * mode + k + 1, :] = (entry * root[k])[0:1]
-            unmix_ref[8 * k + mode : 8 * k + mode + 1, :] = (entry / root[k])[0:1]
+        mix_ref[8 * mode : 8 * mode + 8, :] = flat_v[mode] * scale
+        unmix_ref[pl.ds(mode, 8, stride=8), :] = flat_v[mode] / scale
 
 
 def iota(shape, axis):

time: 115 us -> 114 us (level)
  no operation moved by 1% of the time
where the time goes in v4:
time: 114 us
  blocking collectives  62 us (54%)
  Pallas kernels  28.1 us (25%)
  starting transfers between devices  15.9 us (14%)
  waiting for transfers between devices  6.68 us (6%)
    all_to_all x2, blocking collectives, on_device(): lax.all_to_all(packed, 'gx', split_axis=0, concat_axis=0, tiled=True)  62 us
    all_to_all x1, starting transfers between devices, on_device(): small = lax.all_to_all(small, 'gy', split_axis=0, concat_axis=0, tiled=True)  10.4 us
    pallas_call x1, Pallas kernels, on_device(): pl.pallas_call(forward_kernel, out_shape=(shape((32 * ROWS, 128), f32), s...  9.02 us
    pallas_call x1, Pallas kernels, on_device(): pl.pallas_call(backward_kernel, out_shape=shape(field, f32), in_specs=[SM...  7.29 us
    all_to_all x1, waiting for transfers between devices, on_device(): small = lax.all_to_all(small, 'gy', split_axis=0, concat_axis=0, tiled=True)  6.67 us
    pallas_call x1, Pallas kernels, on_device(): pl.pallas_call(gradient_kernel, out_shape=(out, out, out), grid=(4,), in_...  5.2 us
    ppermute x1, starting transfers between devices, on_device(): lax.ppermute(north, 'gy', [(i, (i - 1) % parts) for i in range(parts)])  5.09 us
    pallas_call x1, Pallas kernels, on_device(): pl.pallas_call(divergence_kernel, out_shape=(shape(field, f32), shape((64...  4.91 us
  transfers between devices with their start and end apart: 3, of which 1 were waited for; matrix products, arithmetic and copies ran while one was open for 0% of the time, Pallas kernels for 1%

profile of v4, /device:TPU:2, one launch (start us, length us, event | category | flops | bytes accessed | tf_op | source)
XLA Modules:
  0.0 114.2 jit_solution(13423964751224641874)
XLA Ops:
  0.6 0.0 copy-start.17
  0.6 0.6 copy-done.17
  1.3 4.9 %divergence.1 = (f32[8,520,128]{2,1,0:T(8,128)S(1)}, f32[64,128]{1,0:T(8,128)S(1)}, f32[8,128]{1,0:T(8,128)S(1)}) custom-call(s32[1]{0:T(128)} %bitcast.gx_ref, f32[8]{0:T(128)S(1)} %copy-done.17, f32[8,512,128]{2,1,0:T(8,128)} %u_ref.1, f32[8,512,128]{2,1,0:T(8,128)} %v_ref.1, f32[8,512,128]{2,1,0:T(8,128)} %w_ref.1), custom_call_target="tpu_custom_call" | custom-call | tf_op jit(solution)/shard_map/divergence/pallas_call | solution.py:723
  6.2 0.0 copy-start.5
  6.2 0.0 copy-start.6
  6.2 0.0 copy-start.7
  6.3 0.0 copy-start.8
  6.3 0.0 copy-start.9
  6.3 32.2 %all_to_all.21.in_ref = f32[8,520,128]{2,1,0:T(8,128)S(1)} all-to-all(f32[8,520,128]{2,1,0:T(8,128)S(1)} %get-tuple-element.12), channel_id=1, replica_groups=mesh['gx'=8,'gy'=32] {'gx'}, dimensions={0} | all-to-all | bytes 4259840 | tf_op jit(solution)/shard_map/all_to_all | solution.py:740
  38.5 0.0 copy-start.10
  38.5 0.0 copy-start.11
  38.5 0.0 copy-start.12
  38.5 0.0 copy-start.13
  38.5 0.0 copy-start.14
  38.5 0.0 copy-start.15
  38.6 0.0 copy-start.16
  38.6 0.0 copy-start.18
  38.6 0.0 copy-start.19
  38.6 0.0 copy-start.3
  38.6 0.0 copy-start.4
  38.6 0.0 copy-done.5
  38.6 0.0 copy-done.6
  38.6 0.0 copy-done.7
  38.6 0.0 copy-done.8
  38.7 0.0 copy-done.9
  38.7 9.0 %forward.1 = (f32[4352,128]{1,0:T(8,128)S(1)}, f32[256,128]{1,0:T(8,128)}, f32[32,128]{1,0:T(8,128)S(1)}, f32[32,128]{1,0:T(8,128)S(1)}) custom-call(s32[1]{0:T(128)} %bitcast.gx_ref, f32[8,128]{1,0:T(8,128)S(1)} %get-tuple-element.11.mu_ref, f32[32,128]{1,0:T(8,128)S(1)} %copy-done.9, f32[32,128]{1,0:T(8,128)S(1)} %copy-done.8, f32[32,128]{1,0:T(8,128)S(1)} %copy-done.7, ...), custom_call_target="tpu_custom_call" | custom-call | tf_op jit(solution)/shard_map/forward/pallas_call | solution.py:743
  47.7 10.4 %all-to-all-start.1 = ((f32[32,8,128]{2,1,0:T(8,128)}), f32[32,8,128]{2,1,0:T(8,128)S(1)}, u32[]{:S(2)}, u32[]{:S(2)}) async-start(f32[32,8,128]{2,1,0:T(8,128)} %bitcast.2), calls=%async_computation.1 | async-start | bytes 262144 | tf_op jit(solution)/shard_map/all_to_all | solution.py:758
  58.1 0.4 collective-permute-start
  58.5 5.1 %collective-permute-start.1 = (f32[32,128]{1,0:T(8,128)S(1)}, f32[32,128]{1,0:T(8,128)S(1)}, u32[]{:S(2)}, u32[]{:S(2)}) collective-permute-start(f32[32,128]{1,0:T(8,128)S(1)} %get-tuple-element.15), channel_id=1, source_target_pairs={{0,31},{1,0},{2,1},{3,2},{4,3},{5,4},{6,5},{7,6},{8,7},{9,8},{10,9... | collective-permute-start | bytes 49160 | tf_op jit(solution)/shard_map/ppermute | solution.py:762
  63.6 6.7 %all-to-all-done.1 = f32[32,8,128]{2,1,0:T(8,128)S(1)} async-done(((f32[32,8,128]{2,1,0:T(8,128)}), f32[32,8,128]{2,1,0:T(8,128)S(1)}, u32[]{:S(2)}, u32[]{:S(2)}) %all-to-all-start.1) | async-done | bytes 131104 | tf_op jit(solution)/shard_map/all_to_all | solution.py:758
  70.2 0.0 copy-done.10
  70.2 0.0 copy-done.11
  70.2 0.0 copy-done.12
  70.2 0.0 copy-done.13
  70.2 0.0 copy-done.14
  70.3 0.0 copy-done.15
  70.3 0.0 copy-done.16
  70.3 0.0 copy-done.18
  70.3 0.0 copy-done.19
  70.3 1.6 %line.1.line_ref = f32[104,128]{1,0:T(8,128)S(1)} custom-call(s32[1]{0:T(128)} %bitcast.gx_ref, s32[1]{0:T(128)} %bitcast.1.gy_ref, f32[8]{0:T(128)S(1)} %copy-done.18, f32[8,128]{1,0:T(8,128)S(1)} %get-tuple-element.11.mu_ref, f32[8,128]{1,0:T(8,128)S(1)} %copy-done.19, f32[32,32]{1,0:T(8,128)S(1)} %copy-done.16, f32[32,32]{1,0:T(8,128)S(1)} %copy-done.15, ...), custom_call_target="tpu_custom_call" | custom-call | tf_op jit(solution)/shard_map/line/pallas_call | solution.py:763
  71.9 0.0 collective-permute-done.south_ref
  72.0 0.0 collective-permute-done.1.north_ref
  72.0 0.0 copy-done.3
  72.0 0.0 copy-done.4
  72.0 0.0 copy-start.2
  72.0 7.3 %backward.1 = f32[8,520,128]{2,1,0:T(8,128)S(1)} custom-call(s32[1]{0:T(128)} %bitcast.gx_ref, s32[1]{0:T(128)} %bitcast.1.gy_ref, f32[8,128]{1,0:T(8,128)S(1)} %get-tuple-element.11.mu_ref, f32[32,128]{1,0:T(8,128)S(1)} %copy-done.9, f32[32,128]{1,0:T(8,128)S(1)} %copy-done.8, f32[32,128]{1,0:T(8,128)S(1)} %copy-done.7, bf16[768,256]{1,0:T(8,128)(2,1)S(1)} %copy-done.4, ...), custom_call_target="tpu_custom_call" | custom-call | tf_op jit(solution)/shard_map/backward/pallas_call | solution.py:773
  79.3 0.0 copy-start
  79.3 0.0 copy-start.1
  79.3 29.7 %all_to_all.22.p_ref = f32[8,520,128]{2,1,0:T(8,128)S(1)} all-to-all(f32[8,520,128]{2,1,0:T(8,128)S(1)} %backward.1), channel_id=1, replica_groups=mesh['gx'=8,'gy'=32] {'gx'}, dimensions={0} | all-to-all | bytes 4259840 | tf_op jit(solution)/shard_map/all_to_all | solution.py:787
  109.0 0.0 copy-done.2
  109.0 0.0 copy-done
  109.0 0.0 copy-done.1
  109.0 5.2 %gradient.1 = (f32[8,512,128]{2,1,0:T(8,128)}, f32[8,512,128]{2,1,0:T(8,128)}, f32[8,512,128]{2,1,0:T(8,128)}) custom-call(s32[1]{0:T(128)} %bitcast.gx_ref, f32[8]{0:T(128)S(1)} %copy-done.18, f32[64,128]{1,0:T(8,128)S(1)} %get-tuple-element.10.unmix_ref, f32[104,128]{1,0:T(8,128)S(1)} %line.1.line_ref, f32[8,520,128]{2,1,0:T(8,128)S(1)} %all_to_all.22.p_ref, ...), custom_call_target="tpu_custom_call" | custom-call | tf_op jit(solution)/shard_map/gradient/pallas_call | solution.py:790
Async XLA Ops:
  0.6 0.7 copy-start.17
  6.2 32.4 %copy-start.5 = (bf16[256,512]{1,0:T(8,128)(2,1)S(1)}, bf16[256,512]{1,0:T(8,128)(2,1)}, u32[]{:S(2)}) copy-start(bf16[256,512]{1,0:T(8,128)(2,1)} %constant.43.clone.first_ref) | copy-start | bytes 786436
  6.2 32.4 %copy-start.6 = (bf16[256,512]{1,0:T(8,128)(2,1)S(1)}, bf16[256,512]{1,0:T(8,128)(2,1)}, u32[]{:S(2)}) copy-start(bf16[256,512]{1,0:T(8,128)(2,1)} %constant.42.clone.common_ref) | copy-start | bytes 786436
  6.2 32.4 %copy-start.7 = (f32[32,128]{1,0:T(8,128)S(1)}, f32[32,128]{1,0:T(8,128)}, u32[]{:S(2)}) copy-start(f32[32,128]{1,0:T(8,128)} %constant.41.clone.ts_ref) | copy-start | bytes 49156
  6.3 32.4 %copy-start.8 = (f32[32,128]{1,0:T(8,128)S(1)}, f32[32,128]{1,0:T(8,128)}, u32[]{:S(2)}) copy-start(f32[32,128]{1,0:T(8,128)} %constant.40.clone.tc_ref) | copy-start | bytes 49156
  6.3 32.4 %copy-start.9 = (f32[32,128]{1,0:T(8,128)S(1)}, f32[32,128]{1,0:T(8,128)}, u32[]{:S(2)}) copy-start(f32[32,128]{1,0:T(8,128)} %constant.39.clone.sines_ref) | copy-start | bytes 49156
  38.5 31.7 %copy-start.10 = (f32[128,128]{1,0:T(8,128)S(1)}, f32[128,128]{1,0:T(8,128)}, u32[]{:S(2)}) copy-start(f32[128,128]{1,0:T(8,128)} %constant.50.clone.s128_ref) | copy-start | bytes 196612
  38.5 31.7 %copy-start.11 = (f32[128,128]{1,0:T(8,128)S(1)}, f32[128,128]{1,0:T(8,128)}, u32[]{:S(2)}) copy-start(f32[128,128]{1,0:T(8,128)} %constant.49.clone.c128_ref) | copy-start | bytes 196612
  38.5 31.7 %copy-start.12 = (f32[32,128]{1,0:T(8,128)S(1)}, f32[32,128]{1,0:T(8,128)}, u32[]{:S(2)}) copy-start(f32[32,128]{1,0:T(8,128)} %constant.51.clone.lam_ref) | copy-start | bytes 49156
  38.5 31.7 %copy-start.13 = (f32[32,128]{1,0:T(8,128)S(1)}, f32[32,128]{1,0:T(8,128)}, u32[]{:S(2)}) copy-start(f32[32,128]{1,0:T(8,128)} %constant.48.clone.ts_ref) | copy-start | bytes 49156
  38.5 31.7 %copy-start.14 = (f32[32,128]{1,0:T(8,128)S(1)}, f32[32,128]{1,0:T(8,128)}, u32[]{:S(2)}) copy-start(f32[32,128]{1,0:T(8,128)} %constant.47.clone.tc_ref) | copy-start | bytes 49156
  38.5 31.7 %copy-start.15 = (f32[32,32]{1,0:T(8,128)S(1)}, f32[32,32]{1,0:T(8,128)}, u32[]{:S(2)}) copy-start(f32[32,32]{1,0:T(8,128)} %constant.46.clone.s32_ref) | copy-start | bytes 12292
  38.6 31.7 %copy-start.16 = (f32[32,32]{1,0:T(8,128)S(1)}, f32[32,32]{1,0:T(8,128)}, u32[]{:S(2)}) copy-start(f32[32,32]{1,0:T(8,128)} %constant.45.clone.c32_ref) | copy-start | bytes 12292
  38.6 31.7 %copy-start.18 = (f32[8]{0:T(128)S(1)}, f32[8]{0:T(128)}, u32[]{:S(2)}) copy-start(f32[8]{0:T(128)} %thick_ref.5) | copy-start | bytes 100
  38.6 31.7 %copy-start.19 = (f32[8,128]{1,0:T(8,128)S(1)}, f32[8,128]{1,0:T(8,128)}, u32[]{:S(2)}) copy-start(f32[8,128]{1,0:T(8,128)} %constant.44.clone.slow_ref) | copy-start | bytes 12292
  38.6 33.4 %copy-start.3 = (bf16[768,256]{1,0:T(8,128)(2,1)S(1)}, bf16[768,256]{1,0:T(8,128)(2,1)}, u32[]{:S(2)}) copy-start(bf16[768,256]{1,0:T(8,128)(2,1)} %constant.53.clone.first_ref) | copy-start | bytes 1179652
  38.6 33.4 %copy-start.4 = (bf16[768,256]{1,0:T(8,128)(2,1)S(1)}, bf16[768,256]{1,0:T(8,128)(2,1)}, u32[]{:S(2)}) copy-start(bf16[768,256]{1,0:T(8,128)(2,1)} %constant.52.clone.common_ref) | copy-start | bytes 1179652
  47.7 22.5 %all-to-all-start.1 = ((f32[32,8,128]{2,1,0:T(8,128)}), f32[32,8,128]{2,1,0:T(8,128)S(1)}, u32[]{:S(2)}, u32[]{:S(2)}) async-start(f32[32,8,128]{2,1,0:T(8,128)} %bitcast.2), calls=%async_computation.1 | async-start | bytes 262144 | tf_op jit(solution)/shard_map/all_to_all | solution.py:758
  58.1 13.8 %collective-permute-start = (f32[32,128]{1,0:T(8,128)S(1)}, f32[32,128]{1,0:T(8,128)S(1)}, u32[]{:S(2)}, u32[]{:S(2)}) collective-permute-start(f32[32,128]{1,0:T(8,128)S(1)} %get-tuple-element.14), channel_id=1, source_target_pairs={{0,1},{1,2},{2,3},{3,4},{4,5},{5,6},{6,7},{7,8},{8,9},{9,10},{10,1... | collective-permute-start | bytes 49160 | tf_op jit(solution)/shard_map/ppermute | solution.py:761
  58.5 13.5 %collective-permute-start.1 = (f32[32,128]{1,0:T(8,128)S(1)}, f32[32,128]{1,0:T(8,128)S(1)}, u32[]{:S(2)}, u32[]{:S(2)}) collective-permute-start(f32[32,128]{1,0:T(8,128)S(1)} %get-tuple-element.15), channel_id=1, source_target_pairs={{0,31},{1,0},{2,1},{3,2},{4,3},{5,4},{6,5},{7,6},{8,7},{9,8},{10,9... | collective-permute-start | bytes 49160 | tf_op jit(solution)/shard_map/ppermute | solution.py:762
  72.0 37.1 %copy-start.2 = (f32[8,512,128]{2,1,0:T(8,128)S(1)}, f32[8,512,128]{2,1,0:T(8,128)}, u32[]{:S(2)}) copy-start(f32[8,512,128]{2,1,0:T(8,128)} %w_ref.1) | copy-start | bytes 6291460
  79.3 29.8 %copy-start = (f32[8,512,128]{2,1,0:T(8,128)S(1)}, f32[8,512,128]{2,1,0:T(8,128)}, u32[]{:S(2)}) copy-start(f32[8,512,128]{2,1,0:T(8,128)} %u_ref.1) | copy-start | bytes 6291460
  79.3 29.7 %copy-start.1 = (f32[8,512,128]{2,1,0:T(8,128)S(1)}, f32[8,512,128]{2,1,0:T(8,128)}, u32[]{:S(2)}) copy-start(f32[8,512,128]{2,1,0:T(8,128)} %v_ref.1) | copy-start | bytes 6291460
